TPU v7x, 512 devices: a whole 4x8x8 slice. The times are simulated.
512 devices in a mesh: region: 16 (over y, core), var: 32 (over z, x).
Axes of the slice: x: 4, y: 8, z: 8, core: 2. Of those that a mesh axis runs over, the one named last changes fastest.
Arguments:
- state: float32 [262144, 768], P(('region', 'var')), may hold values from -6 to 6
- taper: bfloat16 [4, 262144, 384], P(None, ('region', 'var')), may hold values from 0.19921875 to 1
- block_mask: int32 [4, 2048, 3], P(None, ('region', 'var')), may hold values 0 or 1
- anom_fly: float32 [16, 384, 768], P('region', 'var'), may hold values from -6 to 6
- incr_fly: float32 [16, 384, 768], P('region', 'var'), may hold values from -6 to 6
- anom_new: float32 [3, 384, 768], P(None, 'var'), may hold values from -6 to 6
- incr_new: float32 [3, 384, 768], P(None, 'var'), may hold values from -6 to 6
Outputs:
- updated: float32 [262144, 768], P(('region', 'var'))
All inputs are finite; a program needn't handle non-finite values. No bound on the sum of `block_mask` on one device may be relied on, other than what follows from the above.
Results may differ from a plain program's by a relative error of at most 0.0003.
Values sent between devices are 32-bit elements; how exact they have to be, the bound alone decides.
No kernel may reach another device: no remote copies, remote signals or barrier semaphores. Data moves between devices by JAX's collectives and lax.ppermute only.
A program may use at most 64 MiB of HBM per device.

v0:
```python
import jax
import jax.numpy as jnp
from jax import lax
from jax.sharding import PartitionSpec as P

MEMBERS = 768
BLOCK = 128
TICKS = 4


def shifted(block, axis, distance):
    devices = range(lax.axis_size(axis))
    route = [(i - distance, i) for i in devices if i - distance in devices]
    return lax.ppermute(block, axis, route)


def localizer(taper_now, block_flags):
    row_blocks, obs_blocks = block_flags.shape
    expanded = jnp.broadcast_to(
        block_flags[:, None, :, None], (row_blocks, BLOCK, obs_blocks, BLOCK)
    )
    expanded = expanded.reshape(row_blocks * BLOCK, obs_blocks * BLOCK).astype(jnp.float32)
    return taper_now.astype(jnp.float32) * expanded


def assimilate(state_rows, taper_now, block_flags, batch_pair):
    localize = localizer(taper_now, block_flags)
    gathered = lax.all_gather(batch_pair, "var", axis=1, tiled=True)
    covar = lax.dot_general(
        state_rows,
        gathered[0],
        (((1,), (1,)), ((), ())),
        precision=lax.Precision.HIGHEST,
        preferred_element_type=jnp.float32,
    )
    weights = localize * covar / (MEMBERS - 1)
    increment = jnp.dot(
        weights, gathered[1], precision=lax.Precision.HIGHEST, preferred_element_type=jnp.float32
    )
    return state_rows + increment


def on_device(state, taper, block_mask, anom_fly, incr_fly, anom_new, incr_new):
    region_id = lax.axis_index("region")
    in_flight = jnp.stack([anom_fly[0], incr_fly[0]])
    entering = jnp.stack([anom_new, incr_new], 1)
    state_rows = state
    batch_pair = in_flight
    for tick_num in range(TICKS):
        if tick_num > 0:
            arrived = shifted(batch_pair, "region", 1)
            batch_pair = jnp.where(region_id == 0, entering[tick_num - 1], arrived)
        state_rows = assimilate(state_rows, taper[tick_num], block_mask[tick_num], batch_pair)
    return state_rows


def solution(mesh):
    in_specs = (
        P(("region", "var"), None),
        P(None, ("region", "var"), None),
        P(None, ("region", "var"), None),
        P("region", "var", None),
        P("region", "var", None),
        P(None, "var", None),
        P(None, "var", None),
    )
    out_specs = P(("region", "var"), None)
    return jax.shard_map(
        on_device, mesh=mesh, in_specs=in_specs, out_specs=out_specs, check_vma=False
    )
```

profile of v0, /device:TPU:1, one launch (start us, length us, event | category | flops | bytes accessed | tf_op | source)
XLA Modules:
  0.0 365.5 jit_solution(4278995919764913455)
XLA Ops:
  6.5 1.6 pad_maximum_fusion.1
  8.2 0.0 all-gather.7.cloned.1.call-start
  8.2 4.6 %collective-permute-start = (f32[2,12,768]{2,0,1:T(2,128)}, f32[2,12,768]{2,0,1:T(2,128)S(1)}, u32[]{:S(2)}, u32[]{:S(2)}) collective-permute-start(f32[2,12,768]{2,0,1:T(2,128)} %pad_maximum_fusion.1), channel_id=1, source_target_pairs={{0,32},{32,64},{64,96},{96,128},{128,160},{160,192},{192,224},{224... | collective-permute-start | bytes 221192 | tf_op jit(solution)/shard_map/ppermute | solution.py:14
  12.8 1.0 stack.13
  13.8 1.0 stack.14
  14.8 2.5 collective-permute-done
  17.3 0.7 bitcast_select_fusion.1
  18.0 0.0 all-gather.9.cloned.1.call-start
  18.1 1.9 collective-permute-start.1
  20.0 1.7 collective-permute-done.1
  21.7 0.7 bitcast_select_fusion
  22.5 4.2 %collective-permute-start.2 = (f32[2,12,768]{2,0,1:T(2,128)}, f32[2,12,768]{2,0,1:T(2,128)S(1)}, u32[]{:S(2)}, u32[]{:S(2)}) collective-permute-start(f32[2,12,768]{2,0,1:T(2,128)} %bitcast_select_fusion), channel_id=1, source_target_pairs={{0,32},{32,64},{64,96},{96,128},{128,160},{160,192},{192,224},{224... | collective-permute-start | bytes 221192 | tf_op jit(solution)/shard_map/ppermute | solution.py:14
  26.7 1.7 collective-permute-done.2
  28.4 0.7 fusion.24
  29.1 0.2 fusion.29
  29.3 0.2 copy.73
  29.5 0.3 copy-done.3
  29.8 0.1 copy.74
  29.9 0.1 copy.49
  30.0 0.2 copy.75
  30.2 0.1 copy.76
  30.3 0.1 copy.52
  30.4 0.9 copy.77
  31.4 0.1 copy.78
  31.5 0.1 copy.56
  31.6 0.2 copy.79
  31.8 0.1 copy.80
  31.9 0.1 copy.60
  32.0 63.8 %all-gather.5.cloned.1.call-done = f32[2,384,768]{2,0,1:T(2,128)} async-done(((f32[2,12,768]{2,0,1:T(2,128)}), f32[2,384,768]{2,0,1:T(2,128)}) %all-gather.5.cloned.1.call-update) | async-done | bytes 2359312 | tf_op jit(solution)/shard_map/all_gather | solution.py:28
  95.7 4.5 %fusion.28 = (f32[1,384,768]{2,0,1:T(1,128)S(1)}, f32[1,384,768]{2,0,1:T(1,128)S(1)}) fusion(f32[2,384,768]{2,0,1:T(2,128)} %all-gather.5.cloned.1.call-done), kind=kLoop, calls=%fused_computation.52 | loop fusion | bytes 4718592 | tf_op jit(solution)/shard_map/slice | solution.py:38
  100.2 0.2 broadcast_in_dim.8
  100.4 2.1 fusion.1
  102.5 2.9 convolution_add_fusion.3
  105.4 74.4 %all-gather.7.cloned.1.call-done = f32[2,384,768]{2,0,1:T(2,128)} async-done(((f32[2,12,768]{2,0,1:T(2,128)}), f32[2,384,768]{2,0,1:T(2,128)}) %all-gather.7.cloned.1.call-update) | async-done | bytes 2359312 | tf_op jit(solution)/shard_map/all_gather | solution.py:28
  179.9 4.4 %fusion.27 = (f32[1,384,768]{2,0,1:T(1,128)S(1)}, f32[1,384,768]{2,0,1:T(1,128)S(1)}) fusion(f32[2,384,768]{2,0,1:T(2,128)} %all-gather.7.cloned.1.call-done), kind=kLoop, calls=%fused_computation.51 | loop fusion | bytes 4718592 | tf_op jit(solution)/shard_map/slice | solution.py:38
  184.3 0.2 broadcast_in_dim.9
  184.5 2.3 fusion.2
  186.8 2.8 convolution_add_fusion.2
  189.6 74.4 %all-gather.9.cloned.1.call-done = f32[2,384,768]{2,0,1:T(2,128)} async-done(((f32[2,12,768]{2,0,1:T(2,128)}), f32[2,384,768]{2,0,1:T(2,128)}) %all-gather.9.cloned.1.call-update) | async-done | bytes 2359312 | tf_op jit(solution)/shard_map/all_gather | solution.py:28
  264.1 4.4 %fusion.26 = (f32[1,384,768]{2,0,1:T(1,128)S(1)}, f32[1,384,768]{2,0,1:T(1,128)S(1)}) fusion(f32[2,384,768]{2,0,1:T(2,128)} %all-gather.9.cloned.1.call-done), kind=kLoop, calls=%fused_computation.50 | loop fusion | bytes 4718592 | tf_op jit(solution)/shard_map/slice | solution.py:38
  268.5 0.2 broadcast_in_dim.10
  268.6 2.1 fusion.3
  270.8 2.8 convolution_add_fusion.1
  273.6 74.5 %all-gather.11.cloned.1.call-done = f32[2,384,768]{2,0,1:T(2,128)} async-done(((f32[2,12,768]{2,0,1:T(2,128)}), f32[2,384,768]{2,0,1:T(2,128)}) %all-gather.11.cloned.1.call-update) | async-done | bytes 2359312 | tf_op jit(solution)/shard_map/all_gather | solution.py:28
  348.1 4.6 %fusion.25 = (f32[1,384,768]{2,0,1:T(1,128)S(1)}, f32[1,384,768]{2,0,1:T(1,128)S(1)}) fusion(f32[2,384,768]{2,0,1:T(2,128)} %all-gather.11.cloned.1.call-done), kind=kLoop, calls=%fused_computation.49 | loop fusion | bytes 4718592 | tf_op jit(solution)/shard_map/slice | solution.py:38
  352.7 0.2 broadcast_in_dim.11
  352.9 2.1 fusion.4
  355.0 4.0 %convolution_add_fusion = f32[512,768]{1,0:T(8,128)} fusion(f32[512,768]{1,0:T(8,128)S(1)} %convolution_add_fusion.1, f32[512,384]{0,1:T(8,128)S(1)} %fusion.4, f32[1,384,768]{2,0,1:T(1,128)S(1)} %get-tuple-element.5), kind=kOutput, calls=%fused_computation | convolution fusion | flops 1812332544 | bytes 5111808 | tf_op jit(solution)/shard_map/dot_general | solution.py:37
  (18 shorter events, 0.2 us)
Async XLA Ops:
  6.5 22.6 %copy-start.1 = (bf16[4,512,384]{2,1,0:T(8,128)(2,1)S(1)}, bf16[4,512,384]{2,1,0:T(8,128)(2,1)}, u32[]{:S(2)}) copy-start(bf16[4,512,384]{2,1,0:T(8,128)(2,1)} %param.8) | copy-start | bytes 4718596
  6.5 89.2 %all-gather.5.cloned.1.call-start = ((), (), s32[]{:S(2)}) async-start(), calls=%async_computation | async-start | bytes 2433024 | tf_op jit(solution)/shard_map/all_gather | solution.py:28
  8.2 171.7 %all-gather.7.cloned.1.call-start = ((), (), s32[]{:S(2)}) async-start(), calls=%async_computation.1 | async-start | bytes 2433024 | tf_op jit(solution)/shard_map/all_gather | solution.py:28
  8.2 9.1 %collective-permute-start = (f32[2,12,768]{2,0,1:T(2,128)}, f32[2,12,768]{2,0,1:T(2,128)S(1)}, u32[]{:S(2)}, u32[]{:S(2)}) collective-permute-start(f32[2,12,768]{2,0,1:T(2,128)} %pad_maximum_fusion.1), channel_id=1, source_target_pairs={{0,32},{32,64},{64,96},{96,128},{128,160},{160,192},{192,224},{224... | collective-permute-start | bytes 221192 | tf_op jit(solution)/shard_map/ppermute | solution.py:14
  18.0 246.0 %all-gather.9.cloned.1.call-start = ((), (), s32[]{:S(2)}) async-start(), calls=%async_computation.2 | async-start | bytes 2433024 | tf_op jit(solution)/shard_map/all_gather | solution.py:28
  18.1 3.6 collective-permute-start.1
  22.4 325.6 %all-gather.11.cloned.1.call-start = ((), (), s32[]{:S(2)}) async-start(), calls=%async_computation.3 | async-start | bytes 2433024 | tf_op jit(solution)/shard_map/all_gather | solution.py:28
  22.5 5.9 %collective-permute-start.2 = (f32[2,12,768]{2,0,1:T(2,128)}, f32[2,12,768]{2,0,1:T(2,128)S(1)}, u32[]{:S(2)}, u32[]{:S(2)}) collective-permute-start(f32[2,12,768]{2,0,1:T(2,128)} %bitcast_select_fusion), channel_id=1, source_target_pairs={{0,32},{32,64},{64,96},{96,128},{128,160},{160,192},{192,224},{224... | collective-permute-start | bytes 221192 | tf_op jit(solution)/shard_map/ppermute | solution.py:14
  29.1 0.7 copy-start.3
  95.7 4.7 %copy-start = (f32[512,768]{1,0:T(8,128)S(1)}, f32[512,768]{1,0:T(8,128)}, u32[]{:S(2)}) copy-start(f32[512,768]{1,0:T(8,128)} %param.7) | copy-start | bytes 4718596
  189.6 79.0 %copy-start.2 = (bf16[1,512,384]{1,2,0:T(8,128)(2,1)S(1)}, bf16[1,512,384]{1,2,0:T(8,128)(2,1)}, u32[]{:S(2)}) copy-start(bf16[1,512,384]{1,2,0:T(8,128)(2,1)} %copy.77) | copy-start | bytes 1179652
Sparse Core Ops, SparseCore 0:
  10.5 85.1 all-gather.4
  98.9 80.9 all-gather.6
  183.0 80.9 all-gather.8
  267.1 80.9 all-gather.10
where the time goes:
time: 369 us; the launch traced here: 365 us
  waiting for transfers between devices  293 us (79%)
  local copies, waits for them, and re-layouts  23.4 us (6%)
  matrix products  21.1 us (6%)
  between operations  13.3 us (4%)
  starting transfers between devices  10.8 us (3%)
  other arithmetic  3.75 us (1%)
    all_gather x4, waiting for transfers between devices, assimilate(): gathered = lax.all_gather(batch_pair, 'var', axis=1, tiled=True)  287 us
    slice x4, local copies, waits for them, and re-layouts, assimilate(): gathered[1]  17.9 us
    dot_general x4, matrix products, assimilate(): jnp.dot(weights, gathered[1], precision=lax.Precision.HIGHEST, preferred_...  12.4 us
    ppermute x3, starting transfers between devices, shifted(): return lax.ppermute(block, axis, route)  10.7 us
    dot_general x4, matrix products, assimilate(): lax.dot_general(state_rows, gathered[0], (((1,), (1,)), ((), ())), precis...  8.67 us
  transfers between devices with their start and end apart: 7, of which 7 were waited for; matrix products, arithmetic and copies ran while one was open for 10% of the time, Pallas kernels for 0%

commit v1 on v0

v1 whole, which is shorter than its diff:
```python
import functools

import jax
import jax.numpy as jnp
from jax import lax
from jax.experimental import pallas as pl
from jax.experimental.pallas import tpu as pltpu
from jax.sharding import PartitionSpec as P

MEMBERS = 768
HALF = 384
OBS = 384
BLOCK = 128
TICKS = 4
ROWS = 512
SHARE = 12
PACK = 24
SLOTS = 512
N_VAR = 32
N_Y = 8
F32 = jnp.float32
BF16 = jnp.bfloat16


def route(move):
    pairs = []
    for y in range(N_Y):
        for core in range(2):
            for z in range(8):
                for x in range(4):
                    to = move(y, core, z, x)
                    if to is not None:
                        ty, tc, tz, tx = to
                        here = (y * 2 + core) * N_VAR + z * 4 + x
                        there = (ty * 2 + tc) * N_VAR + (tz % 8) * 4 + tx % 4
                        pairs.append((here, there))
    return pairs


def send(block, move):
    return lax.ppermute(block, ("region", "var"), route(move))


def flip(y, core, z, x):
    return y, 1 - core, z, x


def up_y(step):
    return lambda y, core, z, x: (y + step, core, z, x) if y + step < N_Y else None


def packed(anom, incr):
    return jnp.concatenate(
        [anom[..., :8, :], incr[..., :8, :], anom[..., 8:, :], incr[..., 8:, :]], axis=-2
    )


def column_half(block, which):
    return lax.dynamic_slice_in_dim(block, which * HALF, HALF, block.ndim - 1)


def chip_shares(core, y, anom_fly, incr_fly, anom_new, incr_new):
    own = packed(anom_fly[0], incr_fly[0])
    mine = column_half(own, core)
    other = send(column_half(own, 1 - core), flip)
    pair = jnp.stack([jnp.where(core == 1, mine, other), jnp.where(core == 1, other, mine)])
    below = send(pair, up_y(1))
    below2 = send(pair[0], up_y(2))
    fresh = column_half(packed(anom_new, incr_new), core)
    return jnp.stack(
        [
            pair[0],
            pair[1],
            jnp.where(y == 0, fresh[0], below[0]),
            jnp.where(y == 0, fresh[1], below[1]),
            jnp.where(y == 0, fresh[2], jnp.where(y == 1, fresh[0], below2)),
        ]
    )


def slot_table(source):
    slot = jnp.arange(SLOTS)
    part, piece, lane = slot // 256, (slot % 256) // 8, slot % 8
    row = jnp.where(part == 0, lane, 8 + lane)
    obs = source(piece) * SHARE + row
    obs = jnp.where((part == 1) & (lane >= 4), -1, obs)
    return (jnp.arange(OBS)[:, None] == obs[None, :]).astype(BF16)


def localize_kernel(mask_ref, taper_ref, table_ref, out_ref):
    tick = pl.program_id(0)
    for rb in range(ROWS // BLOCK):
        rows = pl.ds(rb * BLOCK, BLOCK)
        parts = []
        for ob in range(OBS // BLOCK):
            flag = mask_ref[(tick * (ROWS // BLOCK) + rb) * (OBS // BLOCK) + ob].astype(F32)
            tile = taper_ref[0, rows, pl.ds(ob * BLOCK, BLOCK)].astype(F32)
            parts.append((tile * flag).astype(BF16))
        kept = jnp.concatenate(parts, axis=1)
        out_ref[0, rows, :] = jnp.dot(kept, table_ref[...], preferred_element_type=F32).astype(BF16)


def localizers(taper, block_mask, table):
    return pl.pallas_call(
        localize_kernel,
        out_shape=jax.ShapeDtypeStruct((TICKS, ROWS, SLOTS), BF16),
        grid_spec=pltpu.PrefetchScalarGridSpec(
            num_scalar_prefetch=1,
            grid=(TICKS,),
            in_specs=[
                pl.BlockSpec((1, ROWS, OBS), lambda t, m: (t, 0, 0)),
                pl.BlockSpec((OBS, SLOTS), lambda t, m: (0, 0)),
            ],
            out_specs=pl.BlockSpec((1, ROWS, SLOTS), lambda t, m: (t, 0, 0)),
        ),
        cost_estimate=pl.CostEstimate(flops=8 * ROWS * OBS * SLOTS, bytes_accessed=4 << 20, transcendentals=0),
        name="localize",
    )(block_mask.reshape(-1), taper, table)


def halves(a):
    hi = a.astype(BF16)
    return hi, (a - hi.astype(F32)).astype(BF16)


def dot3(a, b, dims):
    def one(p, q):
        return lax.dot_general(p, q, (dims, ((), ())), preferred_element_type=F32)

    return one(a[0], b[0]) + one(a[0], b[1]) + one(a[1], b[0])


def tick_kernel(where_ref, state_ref, local_ref, own_ref, par_ref, out_ref):
    core = where_ref[0]
    mine = pl.ds(pl.multiple_of(core * HALF, BLOCK), HALF)
    other = pl.ds(pl.multiple_of((1 - core) * HALF, BLOCK), HALF)

    def rows(ref, part):
        tile = ref[:, 0, 8 * part : 8 * part + 8, :] if len(ref.shape) == 4 else ref[:, 8 * part : 8 * part + 8, :]
        return halves(tile.reshape(256, HALF))

    own = [rows(own_ref, part) for part in range(3)]
    par = [rows(par_ref, part) for part in range(3)]
    for rb in range(2):
        here = pl.ds(rb * 256, 256)
        left, right = state_ref[here, mine], state_ref[here, other]
        x_own, x_par = halves(left), halves(right)
        trans = ((1,), (1,))
        plain = ((1,), (0,))
        cross8 = dot3(x_own, own[0], trans) + dot3(x_par, par[0], trans)
        cross4 = dot3(x_own, own[2], trans) + dot3(x_par, par[2], trans)
        scale = 1.0 / (MEMBERS - 1)
        w8 = local_ref[0, here, :256].astype(F32) * cross8 * scale
        w4 = local_ref[0, here, 256:].astype(F32) * cross4 * scale
        w8, w4 = halves(w8), halves(pltpu.roll(w4, 4, 1))
        out_ref[here, mine] = left + (dot3(w8, own[1], plain) + dot3(w4, own[2], plain))
        out_ref[here, other] = right + (dot3(w8, par[1], plain) + dot3(w4, par[2], plain))


def assimilate(tick, core, state, local, own, par):
    return pl.pallas_call(
        tick_kernel,
        out_shape=jax.ShapeDtypeStruct((ROWS, MEMBERS), F32),
        grid_spec=pltpu.PrefetchScalarGridSpec(
            num_scalar_prefetch=1,
            grid=(1,),
            in_specs=[
                pl.BlockSpec((ROWS, MEMBERS), lambda i, w: (0, 0)),
                pl.BlockSpec((1, ROWS, SLOTS), lambda i, w: (tick, 0, 0)),
                pl.BlockSpec((N_VAR, 1, PACK, HALF), lambda i, w: (0, w[1], 0, 0)),
                pl.BlockSpec((N_VAR, PACK, HALF), lambda i, w: (0, 0, 0)),
            ],
            out_specs=pl.BlockSpec((ROWS, MEMBERS), lambda i, w: (0, 0)),
        ),
        cost_estimate=pl.CostEstimate(flops=12 * ROWS * SLOTS * MEMBERS, bytes_accessed=8 << 20, transcendentals=0),
        name="assimilate",
    )(jnp.stack([core, 1 - core + tick]), state, local, own, par)


def on_device(state, taper, block_mask, anom_fly, incr_fly, anom_new, incr_new):
    region = lax.axis_index("region")
    core, y = region % 2, region // 2
    share = chip_shares(core, y, anom_fly, incr_fly, anom_new, incr_new)
    gathered = lax.all_gather(share, "var", axis=0, tiled=False)
    local = localizers(taper, block_mask, slot_table(lambda piece: piece))
    for tick in range(TICKS):
        give = lax.dynamic_index_in_dim(gathered, tick + core, 1, keepdims=False)
        par = send(give, flip)
        state = assimilate(tick, core, state, local, gathered, par)
    return state


def solution(mesh):
    in_specs = (
        P(("region", "var"), None),
        P(None, ("region", "var"), None),
        P(None, ("region", "var"), None),
        P("region", "var", None),
        P("region", "var", None),
        P(None, "var", None),
        P(None, "var", None),
    )
    return jax.shard_map(
        on_device, mesh=mesh, in_specs=in_specs, out_specs=P(("region", "var"), None), check_vma=False
    )
```

time: 369 us -> 183 us (0.50)
  waiting for transfers between devices: 293 us -> 98.4 us
  Pallas kernels: 0 us -> 36.4 us
  matrix products: 21.1 us -> 0 us
  local copies, waits for them, and re-layouts: 23.4 us -> 9.87 us
  starting transfers between devices: 10.8 us -> 21.7 us
    all_gather x4 -> x1, waiting for transfers between devices: 287 us -> 97.1 us  [on_device(): gathered = lax.all_gather(share, 'var', axis=0, tiled=False)]
    pallas_call x0 -> x5, Pallas kernels: none -> 36.4 us  [the longest x4 31.1 us: assimilate(): pl.pallas_call(tick_kernel, out_shape=jax.ShapeDtypeStruct((ROWS, MEMBERS...]
    dot_general x8 -> x0, matrix products: 21.1 us -> none  [the longest x4 12.4 us: assimilate(): jnp.dot(weights, gathered[1], precision=lax.Precision.HIGHEST, preferred_...]
    slice x6 -> x12, local copies, waits for them, and re-layouts: 18.1 us -> 4.74 us  [the longest x3 1.61 us: packed(): incr[..., 8:, :]]
    ppermute x3 -> x7, starting transfers between devices: 10.7 us -> 21.7 us  [send(): return lax.ppermute(block, ('region', 'var'), route(move))]
    ppermute x3 -> x7, waiting for transfers between devices: 5.9 us -> 1.27 us  [send(): return lax.ppermute(block, ('region', 'var'), route(move))]
    squeeze x0 -> x1, local copies, waits for them, and re-layouts: none -> 3.72 us  [on_device(): give = lax.dynamic_index_in_dim(gathered, tick + core, 1, keepdims=False)]
  transfers between devices with their start and end apart: 7 -> 8, of which waited for: 7 -> 3; matrix products, arithmetic and copies ran while one was open for 10% -> 3% of each run, Pallas kernels for 0% -> 16%
where the time goes in v1:
time: 183 us
  waiting for transfers between devices  98.4 us (54%)
  Pallas kernels  36.4 us (20%)
  starting transfers between devices  21.7 us (12%)
  between operations  13.6 us (7%)
  local copies, waits for them, and re-layouts  9.87 us (5%)
  other arithmetic  2.87 us (2%)
    all_gather x1, waiting for transfers between devices, on_device(): gathered = lax.all_gather(share, 'var', axis=0, tiled=False)  97.1 us
    pallas_call x4, Pallas kernels, assimilate(): pl.pallas_call(tick_kernel, out_shape=jax.ShapeDtypeStruct((ROWS, MEMBERS...  31.1 us
    ppermute x7, starting transfers between devices, send(): return lax.ppermute(block, ('region', 'var'), route(move))  21.7 us
    pallas_call x1, Pallas kernels, localizers(): pl.pallas_call(localize_kernel, out_shape=jax.ShapeDtypeStruct((TICKS, RO...  5.3 us
    squeeze x1, local copies, waits for them, and re-layouts, on_device(): give = lax.dynamic_index_in_dim(gathered, tick + core, 1, keepdims=False)  3.72 us
  transfers between devices with their start and end apart: 8, of which 3 were waited for; matrix products, arithmetic and copies ran while one was open for 3% of the time, Pallas kernels for 16%

profile of v1, /device:TPU:1, one launch (start us, length us, event | category | flops | bytes accessed | tf_op | source)
XLA Modules:
  0.0 182.8 jit_solution(11585536999796813307)
XLA Ops:
  6.5 0.0 slice-start
  6.5 0.0 slice-start.1
  6.5 0.0 all-gather.3.cloned.1.call-start
  6.5 0.8 slice.52
  7.3 0.7 slice.56
  8.0 0.7 slice.54
  8.8 0.7 slice.58
  9.5 8.7 %collective-permute-start = (f32[24,384]{1,0:T(8,128)S(1)}, f32[24,384]{1,0:T(8,128)S(1)}, u32[]{:S(2)}, u32[]{:S(2)}) collective-permute-start(f32[24,384]{1,0:T(8,128)S(1)} %constant_dynamic-slice_fusion), channel_id=1, source_target_pairs={{0,32},{1,33},{2,34},{3,35},{4,36},{5,37},{6,38},{7,39},{8,40},{9,... | collective-permute-start | bytes 110600 | tf_op jit(solution)/shard_map/ppermute | solution.py:41
  18.3 0.9 slice.62
  19.2 0.9 slice.63
  20.1 0.0 collective-permute-done
  20.1 1.3 collective-permute-start.1
  21.4 0.0 slice-done
  21.5 0.0 slice-done.1
  21.5 0.1 fusion.3
  21.6 1.3 collective-permute-start.2
  22.9 0.5 collective-permute-done.1
  23.3 0.8 collective-permute-done.2
  24.1 0.0 copy-start
  24.2 0.7 copy-done
  24.8 0.0 all-gather.3.cloned.1.call-update
  24.8 97.1 %all-gather.3.cloned.1.call-done = f32[160,24,384]{2,1,0:T(8,128)} async-done(((f32[5,24,384]{2,1,0:T(8,128)}), f32[160,24,384]{2,1,0:T(8,128)}) %all-gather.3.cloned.1.call-update) | async-done | bytes 5898256 | tf_op jit(solution)/shard_map/all_gather | solution.py:184
  122.0 0.0 copy-start.1
  122.0 3.7 %dynamic-slice_bitcast_fusion = (f32[32,24,384]{2,1,0:T(8,128)S(1)}, f32[32,24,384]{2,1,0:T(8,128)S(1)}, f32[32,24,384]{2,1,0:T(8,128)S(1)}, f32[32,24,384]{2,1,0:T(8,128)}) fusion(f32[32,5,24,384]{3,2,1,0:T(8,128)} %bitcast.43, s32[]{:T(128)S(6)} %select_n.139, s32[]{:T(128)S(6)} %select_n.138, s32[]{:T(128)S(6)} %select_n.137, s32[]{:T(128)S(6)} %select_n.136), kind=kLoop, calls=%fused_computation | loop fusion | bytes 9437200 | tf_op jit(solution)/shard_map/jit(dynamic_index_in_dim)/squeeze | solution.py:187
  125.7 4.1 %collective-permute-start.3 = (f32[32,24,384]{2,1,0:T(8,128)}, f32[32,24,384]{2,1,0:T(8,128)}, u32[]{:S(2)}, u32[]{:S(2)}) collective-permute-start(f32[32,24,384]{2,1,0:T(8,128)} %get-tuple-element.12), channel_id=1, source_target_pairs={{0,32},{1,33},{2,34},{3,35},{4,36},{5,37},{6,38},{7,39},{8,40},{9,... | collective-permute-start | bytes 3538952 | tf_op jit(solution)/shard_map/ppermute | solution.py:41
  129.8 1.9 %collective-permute-start.4 = (f32[32,24,384]{2,1,0:T(8,128)S(1)}, f32[32,24,384]{2,1,0:T(8,128)}, u32[]{:S(2)}, u32[]{:S(2)}) collective-permute-start(f32[32,24,384]{2,1,0:T(8,128)S(1)} %get-tuple-element.11), channel_id=1, source_target_pairs={{0,32},{1,33},{2,34},{3,35},{4,36},{5,37},{6,38},{7,39},{8,40},{9,... | collective-permute-start | bytes 3538952 | tf_op jit(solution)/shard_map/ppermute | solution.py:41
  131.7 2.4 %collective-permute-start.5 = (f32[32,24,384]{2,1,0:T(8,128)S(1)}, f32[32,24,384]{2,1,0:T(8,128)}, u32[]{:S(2)}, u32[]{:S(2)}) collective-permute-start(f32[32,24,384]{2,1,0:T(8,128)S(1)} %get-tuple-element.10), channel_id=1, source_target_pairs={{0,32},{1,33},{2,34},{3,35},{4,36},{5,37},{6,38},{7,39},{8,40},{9,... | collective-permute-start | bytes 3538952 | tf_op jit(solution)/shard_map/ppermute | solution.py:41
  134.2 1.9 %collective-permute-start.6 = (f32[32,24,384]{2,1,0:T(8,128)S(1)}, f32[32,24,384]{2,1,0:T(8,128)}, u32[]{:S(2)}, u32[]{:S(2)}) collective-permute-start(f32[32,24,384]{2,1,0:T(8,128)S(1)} %get-tuple-element.9), channel_id=1, source_target_pairs={{0,32},{1,33},{2,34},{3,35},{4,36},{5,37},{6,38},{7,39},{8,40},{9,... | collective-permute-start | bytes 3538952 | tf_op jit(solution)/shard_map/ppermute | solution.py:41
  136.1 0.9 fusion.table_ref
  137.0 0.0 copy-done.1
  137.0 0.1 copy.18
  137.1 0.6 reshape.58.mask_ref
  137.7 5.3 %localize.1.local_ref = bf16[4,512,512]{2,1,0:T(8,128)(2,1)} custom-call(s32[48]{0:T(128)} %reshape.58.mask_ref, bf16[4,512,384]{2,1,0:T(8,128)(2,1)} %taper_ref.1, bf16[384,512]{1,0:T(8,128)(2,1)} %fusion.table_ref), custom_call_target="tpu_custom_call" | custom-call | flops 805306368 | bytes 4194304 | tf_op jit(solution)/shard_map/localize/pallas_call | solution.py:104
  143.0 0.6 pad_add_fusion.3.where_ref
  143.6 0.6 pad_add_fusion.2.where_ref
  144.2 0.7 pad_add_fusion
  144.8 0.0 collective-permute-done.3.par_ref
  144.8 7.7 %assimilate.4.state_ref = f32[512,768]{1,0:T(8,128)} custom-call(s32[2]{0:T(128)} %pad_add_fusion.3.where_ref, f32[512,768]{1,0:T(8,128)} %state_ref.1, bf16[4,512,512]{2,1,0:T(8,128)(2,1)} %localize.1.local_ref, f32[32,5,24,384]{3,2,1,0:T(8,128)} %bitcast.44, f32[32,24,384]{2,1,0:T(8,128)} %collective-permute-done.3.par_ref), custom_call_target="tpu_custom_call" | custom-call | flops 2415919104 | bytes 8388608 | tf_op jit(solution)/shard_map/assimilate/pallas_call | solution.py:161
  152.6 0.0 collective-permute-done.4.par_ref
  152.6 7.7 %assimilate.5.state_ref = f32[512,768]{1,0:T(8,128)} custom-call(s32[2]{0:T(128)} %pad_add_fusion.2.where_ref, f32[512,768]{1,0:T(8,128)} %assimilate.4.state_ref, bf16[4,512,512]{2,1,0:T(8,128)(2,1)} %localize.1.local_ref, f32[32,5,24,384]{3,2,1,0:T(8,128)} %bitcast.45, f32[32,24,384]{2,1,0:T(8,128)} %collective-permute-done.4.par_ref), custom_call_target="tpu_custom_call" | custom-call | flops 2415919104 | bytes 8388608 | tf_op jit(solution)/shard_map/assimilate/pallas_call | solution.py:161
  160.3 0.0 collective-permute-done.5.par_ref
  160.3 7.8 %assimilate.6.state_ref = f32[512,768]{1,0:T(8,128)} custom-call(s32[2]{0:T(128)} %get-tuple-element.14.where_ref, f32[512,768]{1,0:T(8,128)} %assimilate.5.state_ref, bf16[4,512,512]{2,1,0:T(8,128)(2,1)} %localize.1.local_ref, f32[32,5,24,384]{3,2,1,0:T(8,128)} %bitcast.46, f32[32,24,384]{2,1,0:T(8,128)} %collective-permute-done.5.par_ref), custom_call_target="tpu_custom_call" | custom-call | flops 2415919104 | bytes 8388608 | tf_op jit(solution)/shard_map/assimilate/pallas_call | solution.py:161
  168.2 0.0 collective-permute-done.6.par_ref
  168.2 7.7 %assimilate.7 = f32[512,768]{1,0:T(8,128)} custom-call(s32[2]{0:T(128)} %get-tuple-element.13.where_ref, f32[512,768]{1,0:T(8,128)} %assimilate.6.state_ref, bf16[4,512,512]{2,1,0:T(8,128)(2,1)} %localize.1.local_ref, f32[32,5,24,384]{3,2,1,0:T(8,128)} %bitcast.47, f32[32,24,384]{2,1,0:T(8,128)} %collective-permute-done.6.par_ref), custom_call_target="tpu_custom_call" | custom-call | flops 2415919104 | bytes 8388608 | tf_op jit(solution)/shard_map/assimilate/pallas_call | solution.py:161
  (11 shorter events, 0.1 us)
Async XLA Ops:
  6.5 14.9 %slice-start = ((f32[3,12,768]{2,1,0:T(8,128)}), f32[3,8,768]{2,1,0:T(8,128)S(1)}, s32[]{:S(2)}) async-start(f32[3,12,768]{2,1,0:T(8,128)} %param.12), calls=%async_computation.1 | async-start | bytes 147456 | tf_op jit(solution)/shard_map/slice | solution.py:54
  6.5 14.9 %slice-start.1 = ((f32[3,12,768]{2,1,0:T(8,128)}), f32[3,8,768]{2,1,0:T(8,128)S(1)}, s32[]{:S(2)}) async-start(f32[3,12,768]{2,1,0:T(8,128)} %param.13), calls=%async_computation.2 | async-start | bytes 147456 | tf_op jit(solution)/shard_map/slice | solution.py:54
  6.5 115.4 %all-gather.3.cloned.1.call-start = ((), (), s32[]{:S(2)}) async-start(), calls=%async_computation | async-start | bytes 6082560 | tf_op jit(solution)/shard_map/all_gather | solution.py:184
  9.5 10.6 %collective-permute-start = (f32[24,384]{1,0:T(8,128)S(1)}, f32[24,384]{1,0:T(8,128)S(1)}, u32[]{:S(2)}, u32[]{:S(2)}) collective-permute-start(f32[24,384]{1,0:T(8,128)S(1)} %constant_dynamic-slice_fusion), channel_id=1, source_target_pairs={{0,32},{1,33},{2,34},{3,35},{4,36},{5,37},{6,38},{7,39},{8,40},{9,... | collective-permute-start | bytes 110600 | tf_op jit(solution)/shard_map/ppermute | solution.py:41
  20.1 3.2 %collective-permute-start.1 = (f32[2,24,384]{2,1,0:T(8,128)S(1)}, f32[2,24,384]{2,1,0:T(8,128)S(1)}, u32[]{:S(2)}, u32[]{:S(2)}) collective-permute-start(f32[2,24,384]{2,1,0:T(8,128)S(1)} %pad_maximum_fusion.1), channel_id=1, source_target_pairs={{0,64},{1,65},{2,66},{3,67},{4,68},{5,69},{6,70},{7,71},{8,72},{9,... | collective-permute-start | bytes 221192 | tf_op jit(solution)/shard_map/ppermute | solution.py:41
  21.6 2.6 %collective-permute-start.2 = (f32[24,384]{1,0:T(8,128)S(1)}, f32[24,384]{1,0:T(8,128)S(1)}, u32[]{:S(2)}, u32[]{:S(2)}) collective-permute-start(f32[24,384]{1,0:T(8,128)S(1)} %get-tuple-element.8), channel_id=1, source_target_pairs={{0,128},{1,129},{2,130},{3,131},{4,132},{5,133},{6,134},{7,135},{8... | collective-permute-start | bytes 110600 | tf_op jit(solution)/shard_map/ppermute | solution.py:41
  24.1 0.7 copy-start
  122.0 15.0 %copy-start.1 = (s32[4,4,3]{1,0,2:T(4,128)S(1)}, s32[4,4,3]{1,0,2:T(4,128)}, u32[]{:S(2)}) copy-start(s32[4,4,3]{1,0,2:T(4,128)} %param.9) | copy-start | bytes 580
  125.7 19.1 %collective-permute-start.3 = (f32[32,24,384]{2,1,0:T(8,128)}, f32[32,24,384]{2,1,0:T(8,128)}, u32[]{:S(2)}, u32[]{:S(2)}) collective-permute-start(f32[32,24,384]{2,1,0:T(8,128)} %get-tuple-element.12), channel_id=1, source_target_pairs={{0,32},{1,33},{2,34},{3,35},{4,36},{5,37},{6,38},{7,39},{8,40},{9,... | collective-permute-start | bytes 3538952 | tf_op jit(solution)/shard_map/ppermute | solution.py:41
  129.8 22.8 %collective-permute-start.4 = (f32[32,24,384]{2,1,0:T(8,128)S(1)}, f32[32,24,384]{2,1,0:T(8,128)}, u32[]{:S(2)}, u32[]{:S(2)}) collective-permute-start(f32[32,24,384]{2,1,0:T(8,128)S(1)} %get-tuple-element.11), channel_id=1, source_target_pairs={{0,32},{1,33},{2,34},{3,35},{4,36},{5,37},{6,38},{7,39},{8,40},{9,... | collective-permute-start | bytes 3538952 | tf_op jit(solution)/shard_map/ppermute | solution.py:41
  131.7 28.6 %collective-permute-start.5 = (f32[32,24,384]{2,1,0:T(8,128)S(1)}, f32[32,24,384]{2,1,0:T(8,128)}, u32[]{:S(2)}, u32[]{:S(2)}) collective-permute-start(f32[32,24,384]{2,1,0:T(8,128)S(1)} %get-tuple-element.10), channel_id=1, source_target_pairs={{0,32},{1,33},{2,34},{3,35},{4,36},{5,37},{6,38},{7,39},{8,40},{9,... | collective-permute-start | bytes 3538952 | tf_op jit(solution)/shard_map/ppermute | solution.py:41
  134.2 34.0 %collective-permute-start.6 = (f32[32,24,384]{2,1,0:T(8,128)S(1)}, f32[32,24,384]{2,1,0:T(8,128)}, u32[]{:S(2)}, u32[]{:S(2)}) collective-permute-start(f32[32,24,384]{2,1,0:T(8,128)S(1)} %get-tuple-element.9), channel_id=1, source_target_pairs={{0,32},{1,33},{2,34},{3,35},{4,36},{5,37},{6,38},{7,39},{8,40},{9,... | collective-permute-start | bytes 3538952 | tf_op jit(solution)/shard_map/ppermute | solution.py:41
Sparse Core Ops, SparseCore 0:
  25.0 96.9 all-gather.2

commit v2 on v1

v2 whole, which is shorter than its diff:
```python
import jax
import jax.numpy as jnp
import numpy as np
from jax import lax
from jax.experimental import pallas as pl
from jax.experimental.pallas import tpu as pltpu
from jax.sharding import PartitionSpec as P

MEMBERS = 768
HALF = 384
OBS = 384
BLOCK = 128
TICKS = 4
ROWS = 512
SHARE = 12
PACK = 24
SLOTS = 384
N_VAR = 32
N_Y = 8
F32 = jnp.float32
BF16 = jnp.bfloat16


def route(move):
    pairs = []
    for y in range(N_Y):
        for core in range(2):
            for z in range(8):
                for x in range(4):
                    to = move(y, core, z, x)
                    if to is not None:
                        ty, tc, tz, tx = to
                        here = (y * 2 + core) * N_VAR + z * 4 + x
                        there = (ty * 2 + tc) * N_VAR + (tz % 8) * 4 + tx % 4
                        pairs.append((here, there))
    return pairs


def send(block, move):
    return lax.ppermute(block, ("region", "var"), route(move))


def flip(y, core, z, x):
    return y, 1 - core, z, x


def up_y(step):
    return lambda y, core, z, x: (y + step, core, z, x) if y + step < N_Y else None


def pack_kernel(core_ref, anom_ref, incr_ref, anom_new_ref, incr_new_ref, mine_ref, other_ref, fresh_ref):
    core = core_ref[0]
    for col in range(HALF // BLOCK):
        to = slice(col * BLOCK, (col + 1) * BLOCK)
        for half, out_ref in ((core, mine_ref), (1 - core, other_ref)):
            lane = half * (HALF // BLOCK) + col
            anom = anom_ref[pl.ds(lane, SHARE, stride=MEMBERS // BLOCK), :]
            incr = incr_ref[pl.ds(lane, SHARE, stride=MEMBERS // BLOCK), :]
            out_ref[0:8, to], out_ref[8:16, to] = anom[:8], incr[:8]
            out_ref[16:20, to], out_ref[20:24, to] = anom[8:], incr[8:]
    mine = pl.ds(pl.multiple_of(core * HALF, BLOCK), HALF)
    for batch in range(3):
        fresh_ref[batch, 0:8] = anom_new_ref[batch, 0:8, mine]
        fresh_ref[batch, 8:16] = incr_new_ref[batch, 0:8, mine]
        fresh_ref[batch, 16:20] = anom_new_ref[batch, 8:12, mine]
        fresh_ref[batch, 20:24] = incr_new_ref[batch, 8:12, mine]


def share_kernel(where_ref, pair_ref, below_ref, below2_ref, fresh_ref, out_ref):
    y = where_ref[0]
    out_ref[0:2] = pair_ref[...]
    out_ref[2:4] = jnp.where(y == 0, fresh_ref[0:2], below_ref[...])
    out_ref[4] = jnp.where(y == 0, fresh_ref[2], jnp.where(y == 1, fresh_ref[0], below2_ref[...]))


def pair_kernel(core_ref, mine_ref, other_ref, out_ref):
    out_ref[1 - core_ref[0]] = mine_ref[...]
    out_ref[core_ref[0]] = other_ref[...]


def small_call(kernel, name, out_shape, scalar, *arrays):
    vmem = pl.BlockSpec(memory_space=pltpu.VMEM)
    many = isinstance(out_shape[0], tuple)
    shapes = tuple(jax.ShapeDtypeStruct(o, F32) for o in (out_shape if many else (out_shape,)))
    return pl.pallas_call(
        kernel,
        out_shape=shapes if many else shapes[0],
        in_specs=[pl.BlockSpec(memory_space=pltpu.SMEM)] + [vmem] * len(arrays),
        out_specs=(vmem,) * len(shapes) if many else vmem,
        name=name,
    )(scalar.reshape(1), *arrays)


def chip_shares(core, y, anom_fly, incr_fly, anom_new, incr_new):
    flat = (SHARE * MEMBERS // BLOCK, BLOCK)
    tile = (PACK, HALF)
    mine, give, fresh = small_call(
        pack_kernel, "pack", (tile, tile, (3, *tile)), core,
        anom_fly.reshape(flat), incr_fly.reshape(flat), anom_new, incr_new,
    )
    other = send(give, flip)
    pair = small_call(pair_kernel, "pair", (2, *tile), core, mine, other)
    below = send(pair, up_y(1))
    below2 = send(pair[0], up_y(2))
    return small_call(share_kernel, "share", (5, *tile), y, pair, below, below2, fresh)


FAR_Z = (0, 1, -1, 2, -2, 3, -3, 4)
FAR_X = (0, 1, -1, 2)


def piece_order():
    first = [(dz, dx) for dz in (0, 4, 1, -1, 2, -2, 3, -3) for dx in FAR_X]
    second = []
    for dx, part in ((0, 0), (0, 1), (1, 0), (-1, 0), (1, 1), (-1, 1), (2, 0), (2, 1)):
        second += [(dz, dx) for dz in FAR_Z[4 * part : 4 * part + 4]]
    return first, second


ORDER = piece_order()
PARTNER = tuple(tuple(ORDER[1 - core].index(piece) for piece in ORDER[core]) for core in range(2))


def both(to_first, to_second):
    def move(y, core, z, x):
        way = (to_first, to_second)[core]
        return None if way is None else (y, core, z + way[0], x + way[1])

    return move


def hold(value, *others):
    return lax.optimization_barrier((value, *others))[0]


def gather_pieces(core, share, local):
    first = core == 0
    up, down = both((1, 0), (0, 1)), both((-1, 0), (0, -1))
    near_up, near_down = both((0, 1), (1, 0)), both((0, -1), (-1, 0))
    to_second = lambda y, core, z, x: (y, 1, z, x) if core == 0 else None
    to_first = lambda y, core, z, x: (y, 0, z, x) if core == 1 else None
    n1 = send(share, near_up)
    n2 = send(share, near_down)
    n3 = send(n1, near_up)
    low = jnp.stack([share, n1, n2, n3])
    up1 = send(low, up)
    down1 = send(low, down)
    only_up, only_down = both(None, (1, 0)), both(None, (-1, 0))
    n4 = send(n2, only_down)
    n5 = send(n3, only_up)
    n6 = send(n4, only_down)
    n7 = send(n5, only_up)
    high = jnp.stack([n4, n5, n6, n7])
    up2 = send(hold(jnp.where(first, up1, high), local), up)
    down2 = send(jnp.where(first, down1, high), down)
    up3 = send(jnp.where(first, up2, up1), up)
    down3 = send(down2, down)
    par_low, par_up1, par_down1 = (send(hold(block, up2), flip) for block in (low, up1, down1))
    par_high = send(hold(high, up2), to_first)
    far_up = send(up3[:2], both((1, 0), None))
    far_down = send(down3[2:], both((-1, 0), None))
    par_up2, par_down2 = send(hold(up2, up3), flip), send(hold(down2, up3), flip)
    par_up3, par_down3 = send(hold(up3, down3), flip), send(down3, flip)
    par_far_up, par_far_down = send(far_up, to_second), send(far_down, to_second)
    own = [low, up1, down1, up2, down2, up3, down3, far_up, far_down, high]
    par = [par_low, par_up1, par_down1, par_up2, par_down2, par_up3, par_down3, par_far_up, par_far_down, par_high]
    return own, par


def slot_table(core, z, x):
    far = jnp.asarray(np.array(ORDER, np.int32))[core]
    source = ((z - far[:, 0]) % 8) * 4 + (x - far[:, 1]) % 4
    lane = jnp.arange(SHARE)
    rows = source[:, None] * SHARE + lane[None, :]
    obs = jnp.concatenate([rows[:, :8].reshape(-1), rows[:, 8:].reshape(-1)])
    return (jnp.arange(OBS)[:, None] == obs[None, :]).astype(BF16)


def localize_kernel(mask_ref, taper_ref, table_ref, out_ref):
    tick = pl.program_id(0)
    for rb in range(ROWS // BLOCK):
        rows = pl.ds(rb * BLOCK, BLOCK)
        parts = []
        for ob in range(OBS // BLOCK):
            flag = mask_ref[(tick * (ROWS // BLOCK) + rb) * (OBS // BLOCK) + ob].astype(F32)
            tile = taper_ref[0, rows, pl.ds(ob * BLOCK, BLOCK)].astype(F32)
            parts.append((tile * flag).astype(BF16))
        kept = jnp.concatenate(parts, axis=1)
        out_ref[0, rows, :] = jnp.dot(kept, table_ref[...], preferred_element_type=F32).astype(BF16)


def localizers(taper, block_mask, table):
    return pl.pallas_call(
        localize_kernel,
        out_shape=jax.ShapeDtypeStruct((TICKS, ROWS, SLOTS), BF16),
        grid_spec=pltpu.PrefetchScalarGridSpec(
            num_scalar_prefetch=1,
            grid=(TICKS,),
            in_specs=[
                pl.BlockSpec((1, ROWS, OBS), lambda t, m: (t, 0, 0)),
                pl.BlockSpec((OBS, SLOTS), lambda t, m: (0, 0)),
            ],
            out_specs=pl.BlockSpec((1, ROWS, SLOTS), lambda t, m: (t, 0, 0)),
        ),
        cost_estimate=pl.CostEstimate(flops=8 * ROWS * OBS * SLOTS, bytes_accessed=4 << 20, transcendentals=0),
        name="localize",
    )(block_mask.reshape(-1), taper, table)


def halves(a):
    hi = a.astype(BF16)
    return hi, (a - hi.astype(F32)).astype(BF16)


def dot3(a, b, dims):
    def one(p, q):
        return lax.dot_general(p, q, (dims, ((), ())), preferred_element_type=F32)

    return one(a[0], b[0]) + one(a[0], b[1]) + one(a[1], b[0])


def ticks_kernel(where_ref, state_ref, local_ref, *refs):
    own_refs, par_refs, out_ref, own_rows, par_rows = refs[:10], refs[10:20], refs[20], refs[21:25], refs[25:29]
    core = where_ref[0]
    mine = pl.ds(pl.multiple_of(core * HALF, BLOCK), HALF)
    other = pl.ds(pl.multiple_of((1 - core) * HALF, BLOCK), HALF)

    @pl.when(pl.program_id(0) == 0)
    def _():
        out_ref[...] = state_ref[...]

    def piece(held, at, of_first):
        array, part = at // 4, at % 4
        if array == 1 and of_first:
            return held[7 + part // 2][part % 2, 0]
        return held[9 if array == 1 else max(array - 1, 0)][part, 0]

    def put(rows, at, anom, incr):
        for (hi, lo), value in ((rows[:2], anom), (rows[2:], incr)):
            hi[at : at + 16], lo[at : at + 16] = halves(value)

    upper = lax.broadcasted_iota(jnp.int32, (8, HALF), 0) < 4

    def arrange(rows, pieces):
        for at in range(0, N_VAR, 4):
            four = pieces(at)
            for k in (0, 2):
                pair = four[k : k + 2]
                put(
                    rows,
                    8 * (at + k),
                    jnp.concatenate([p[0:8] for p in pair], axis=0),
                    jnp.concatenate([p[8:16] for p in pair], axis=0),
                )
            rest = [p[16:24] for p in four]
            turned = [pltpu.roll(p, 4, 0) for p in rest]
            put(
                rows,
                256 + 4 * at,
                jnp.concatenate([jnp.where(upper, rest[k], turned[k + 1]) for k in (0, 2)], axis=0),
                jnp.concatenate([jnp.where(upper, turned[k], rest[k + 1]) for k in (0, 2)], axis=0),
            )

    for me in range(2):

        @pl.when(core == me)
        def _(me=me):
            arrange(own_rows, lambda at: [piece(own_refs, at + k, me == 0) for k in range(4)])
            arrange(par_rows, lambda at: [piece(par_refs, PARTNER[me][at + k], me == 1) for k in range(4)])

    def both_parts(rows, first):
        return rows[first][...], rows[first + 1][...]

    trans, plain = ((1,), (1,)), ((1,), (0,))
    left, right = out_ref[:, mine], out_ref[:, other]
    cross = dot3(halves(left), both_parts(own_rows, 0), trans) + dot3(halves(right), both_parts(par_rows, 0), trans)
    weight = halves(local_ref[0].astype(F32) * cross * (1.0 / (MEMBERS - 1)))
    out_ref[:, mine] = left + dot3(weight, both_parts(own_rows, 2), plain)
    out_ref[:, other] = right + dot3(weight, both_parts(par_rows, 2), plain)


def run_ticks(core, state, local, own, par):
    four, two = (
        pl.BlockSpec((n, 1, PACK, HALF), lambda t, w: (0, 1 - w[0] + t, 0, 0)) for n in (4, 2)
    )
    return pl.pallas_call(
        ticks_kernel,
        out_shape=jax.ShapeDtypeStruct((ROWS, MEMBERS), F32),
        grid_spec=pltpu.PrefetchScalarGridSpec(
            num_scalar_prefetch=1,
            grid=(TICKS,),
            in_specs=[
                pl.BlockSpec((ROWS, MEMBERS), lambda t, w: (0, 0)),
                pl.BlockSpec((1, ROWS, SLOTS), lambda t, w: (t, 0, 0)),
            ]
            + ([four] * 7 + [two] * 2 + [four]) * 2,
            out_specs=pl.BlockSpec((ROWS, MEMBERS), lambda t, w: (0, 0)),
            scratch_shapes=[pltpu.VMEM((OBS, HALF), BF16)] * 8,
        ),
        cost_estimate=pl.CostEstimate(flops=48 * ROWS * SLOTS * MEMBERS, bytes_accessed=16 << 20, transcendentals=0),
        name="ticks",
    )(core.reshape(1), state, local, *own, *par)


def on_device(state, taper, block_mask, anom_fly, incr_fly, anom_new, incr_new):
    region, place = lax.axis_index("region"), lax.axis_index("var")
    core, y = region % 2, region // 2
    share = chip_shares(core, y, anom_fly, incr_fly, anom_new, incr_new)
    local = localizers(taper, block_mask, slot_table(core, place // 4, place % 4))
    own, par = gather_pieces(core, share, local)
    return run_ticks(core, state, local, own, par)


def solution(mesh):
    in_specs = (
        P(("region", "var"), None),
        P(None, ("region", "var"), None),
        P(None, ("region", "var"), None),
        P("region", "var", None),
        P("region", "var", None),
        P(None, "var", None),
        P(None, "var", None),
    )
    return jax.shard_map(
        on_device, mesh=mesh, in_specs=in_specs, out_specs=P(("region", "var"), None), check_vma=False
    )
```

time: 183 us -> 143 us (0.78)
  waiting for transfers between devices: 98.4 us -> 18.4 us
  starting transfers between devices: 21.7 us -> 84.6 us
  between operations: 13.6 us -> 0.68 us
  Pallas kernels: 36.4 us -> 30.1 us
  local copies, waits for them, and re-layouts: 9.87 us -> 5.4 us
    all_gather x1 -> x0, waiting for transfers between devices: 97.1 us -> none  [on_device(): gathered = lax.all_gather(share, 'var', axis=0, tiled=False)]
    ppermute x7 -> x28, starting transfers between devices: 21.7 us -> 84.6 us  [send(): return lax.ppermute(block, ('region', 'var'), route(move))]
    ppermute x7 -> x28, waiting for transfers between devices: 1.27 us -> 18.4 us  [send(): return lax.ppermute(block, ('region', 'var'), route(move))]
    pallas_call x4, Pallas kernels: 31.1 us -> 24.9 us  [the longest x1 20.1 us: run_ticks(): pl.pallas_call(ticks_kernel, out_shape=jax.ShapeDtypeStruct((ROWS, MEMBER...]
    slice x12 -> x3, local copies, waits for them, and re-layouts: 4.74 us -> 0.12 us  [the longest x1 0.07 us: slot_table(): obs = jnp.concatenate([rows[:, :8].reshape(-1), rows[:, 8:].reshape(-1)])]
    squeeze x1 -> x2, local copies, waits for them, and re-layouts: 3.72 us -> 1.47 us  [the longest x1 0.78 us: chip_shares(): below2 = send(pair[0], up_y(2))]
    unnamed x5 -> x49, local copies, waits for them, and re-layouts: 0.78 us -> 3 us
  transfers between devices with their start and end apart: 8 -> 28, of which waited for: 3 -> 8; matrix products, arithmetic and copies ran while one was open for 3% -> 2% of each run, Pallas kernels for 16% -> 4%
where the time goes in v2:
time: 143 us; the launch traced here: 141 us
  starting transfers between devices  84.6 us (59%)
  Pallas kernels  30.1 us (21%)
  waiting for transfers between devices  18.4 us (13%)
  local copies, waits for them, and re-layouts  5.4 us (4%)
  other arithmetic  2.12 us (1%)
    ppermute x28, starting transfers between devices, send(): return lax.ppermute(block, ('region', 'var'), route(move))  84.6 us
    pallas_call x1, Pallas kernels, run_ticks(): pl.pallas_call(ticks_kernel, out_shape=jax.ShapeDtypeStruct((ROWS, MEMBER...  20.1 us
    ppermute x28, waiting for transfers between devices, send(): return lax.ppermute(block, ('region', 'var'), route(move))  18.4 us
    pallas_call x1, Pallas kernels, localizers(): pl.pallas_call(localize_kernel, out_shape=jax.ShapeDtypeStruct((TICKS, RO...  5.15 us
    pallas_call x3, Pallas kernels, small_call(): pl.pallas_call(kernel, out_shape=shapes if many else shapes[0], in_specs=...  4.83 us
    unnamed x49, local copies, waits for them, and re-layouts  3 us
  transfers between devices with their start and end apart: 28, of which 8 were waited for; matrix products, arithmetic and copies ran while one was open for 2% of the time, Pallas kernels for 4%

profile of v2, /device:TPU:1, one launch (start us, length us, event | category | flops | bytes accessed | tf_op | source)
XLA Modules:
  0.0 141.3 jit_solution(2571900303284596433)
XLA Ops:
  0.0 1.7 %pack.1 = (f32[24,384]{1,0:T(8,128)}, f32[24,384]{1,0:T(8,128)}, f32[3,24,384]{2,1,0:T(8,128)}) custom-call(s32[1]{0:T(128)} %bitcast.core_ref.where_ref, f32[72,128]{1,0:T(8,128)} %bitcast.28, f32[72,128]{1,0:T(8,128)} %bitcast.29, f32[3,12,768]{2,1,0:T(8,128)} %anom_new_ref.1, f32[3,12,768]{2,1,0:T(8,128)} %incr_new_ref.1), custom_call_target="tpu_custom_call" | custom-call | tf_op jit(solution)/shard_map/pack/pallas_call | solution.py:85
  1.7 8.7 %collective-permute-start = (f32[24,384]{1,0:T(8,128)}, f32[24,384]{1,0:T(8,128)S(1)}, u32[]{:S(2)}, u32[]{:S(2)}) collective-permute-start(f32[24,384]{1,0:T(8,128)} %get-tuple-element.17), channel_id=1, source_target_pairs={{0,32},{1,33},{2,34},{3,35},{4,36},{5,37},{6,38},{7,39},{8,40},{9,... | collective-permute-start | bytes 110600 | tf_op jit(solution)/shard_map/ppermute | solution.py:40
  10.5 1.1 collective-permute-done.other_ref
  12.1 1.4 %pair.1.pair_ref = f32[2,24,384]{2,1,0:T(8,128)} custom-call(s32[1]{0:T(128)} %bitcast.core_ref.where_ref, f32[24,384]{1,0:T(8,128)} %get-tuple-element.16.mine_ref, f32[24,384]{1,0:T(8,128)} %copy-done.10), custom_call_target="tpu_custom_call" | custom-call | tf_op jit(solution)/shard_map/pair/pallas_call | solution.py:85
  13.6 1.3 collective-permute-start.1
  14.8 0.8 slice_bitcast_fusion
  15.6 1.3 collective-permute-start.2
  16.9 1.0 collective-permute-done.2.below2_ref
  18.0 0.6 copy-done.9
  18.6 1.7 %share.1 = f32[5,24,384]{2,1,0:T(8,128)} custom-call(s32[1]{0:T(128)} %bitcast.3.where_ref, f32[2,24,384]{2,1,0:T(8,128)} %pair.1.pair_ref, f32[2,24,384]{2,1,0:T(8,128)} %copy-done.8, f32[24,384]{1,0:T(8,128)} %copy-done.9, f32[3,24,384]{2,1,0:T(8,128)} %get-tuple-element.18.fresh_ref), custom_call_target="tpu_custom_call" | custom-call | tf_op jit(solution)/shard_map/share/pallas_call | solution.py:85
  20.3 3.5 %collective-permute-start.3 = (f32[5,24,384]{2,1,0:T(8,128)}, f32[5,24,384]{2,1,0:T(8,128)S(1)}, u32[]{:S(2)}, u32[]{:S(2)}) collective-permute-start(f32[5,24,384]{2,1,0:T(8,128)} %share.1), channel_id=1, source_target_pairs={{0,1},{1,2},{2,3},{3,0},{4,5},{5,6},{6,7},{7,4},{8,9},{9,10},{10,1... | collective-permute-start | bytes 552968 | tf_op jit(solution)/shard_map/ppermute | solution.py:40
  23.8 8.6 %collective-permute-start.4 = (f32[5,24,384]{2,1,0:T(8,128)}, f32[5,24,384]{2,1,0:T(8,128)S(1)}, u32[]{:S(2)}, u32[]{:S(2)}) collective-permute-start(f32[5,24,384]{2,1,0:T(8,128)} %share.1), channel_id=1, source_target_pairs={{0,3},{1,0},{2,1},{3,2},{4,7},{5,4},{6,5},{7,6},{8,11},{9,8},{10,9... | collective-permute-start | bytes 552968 | tf_op jit(solution)/shard_map/ppermute | solution.py:40
  32.4 1.2 collective-permute-done.3
  33.6 1.9 %collective-permute-start.5 = (f32[5,24,384]{2,1,0:T(8,128)S(1)}, f32[5,24,384]{2,1,0:T(8,128)S(1)}, u32[]{:S(2)}, u32[]{:S(2)}) collective-permute-start(f32[5,24,384]{2,1,0:T(8,128)S(1)} %collective-permute-done.3), channel_id=1, source_target_pairs={{0,1},{1,2},{2,3},{3,0},{4,5},{5,6},{6,7},{7,4},{8,9},{9,10},{10,1... | collective-permute-start | bytes 552968 | tf_op jit(solution)/shard_map/ppermute | solution.py:40
  35.5 0.7 dynamic-slice_bitcast_fusion
  36.2 4.8 %collective-permute-done.5 = f32[5,24,384]{2,1,0:T(8,128)S(1)} collective-permute-done((f32[5,24,384]{2,1,0:T(8,128)S(1)}, f32[5,24,384]{2,1,0:T(8,128)S(1)}, u32[]{:S(2)}, u32[]{:S(2)}) %collective-permute-start.5) | collective-permute-done | bytes 184352 | tf_op jit(solution)/shard_map/ppermute | solution.py:40
  41.0 1.0 pad_maximum_fusion.refs_0_
  42.0 4.4 %collective-permute-start.7 = (f32[4,5,24,384]{3,2,1,0:T(8,128)S(1)}, f32[4,5,24,384]{3,2,1,0:T(8,128)S(1)}, u32[]{:S(2)}, u32[]{:S(2)}) collective-permute-start(f32[4,5,24,384]{3,2,1,0:T(8,128)S(1)} %pad_maximum_fusion.refs_0_), channel_id=1, source_target_pairs={{0,28},{1,29},{2,30},{3,31},{4,0},{5,1},{6,2},{7,3},{8,4},{9,5},{1... | collective-permute-start | bytes 2211848 | tf_op jit(solution)/shard_map/ppermute | solution.py:40
  46.4 1.9 %collective-permute-start.6 = (f32[4,5,24,384]{3,2,1,0:T(8,128)S(1)}, f32[4,5,24,384]{3,2,1,0:T(8,128)S(1)}, u32[]{:S(2)}, u32[]{:S(2)}) collective-permute-start(f32[4,5,24,384]{3,2,1,0:T(8,128)S(1)} %pad_maximum_fusion.refs_0_), channel_id=1, source_target_pairs={{0,4},{1,5},{2,6},{3,7},{4,8},{5,9},{6,10},{7,11},{8,12},{9,13},{1... | collective-permute-start | bytes 2211848 | tf_op jit(solution)/shard_map/ppermute | solution.py:40
  48.4 2.4 %collective-permute-start.8 = (f32[5,24,384]{2,1,0:T(8,128)S(1)}, f32[5,24,384]{2,1,0:T(8,128)S(1)}, u32[]{:S(2)}, u32[]{:S(2)}) collective-permute-start(f32[5,24,384]{2,1,0:T(8,128)S(1)} %collective-permute-done.4), channel_id=1, source_target_pairs={{32,60},{33,61},{34,62},{35,63},{36,32},{37,33},{38,34},{39,35},{4... | collective-permute-start | bytes 552968 | tf_op jit(solution)/shard_map/ppermute | solution.py:40
  50.8 2.8 %collective-permute-start.9 = (f32[5,24,384]{2,1,0:T(8,128)S(1)}, f32[5,24,384]{2,1,0:T(8,128)S(1)}, u32[]{:S(2)}, u32[]{:S(2)}) collective-permute-start(f32[5,24,384]{2,1,0:T(8,128)S(1)} %collective-permute-done.5), channel_id=1, source_target_pairs={{32,36},{33,37},{34,38},{35,39},{36,40},{37,41},{38,42},{39,43},{4... | collective-permute-start | bytes 552968 | tf_op jit(solution)/shard_map/ppermute | solution.py:40
  53.9 0.6 reshape.26.mask_ref
  55.2 5.3 %collective-permute-start.10 = (f32[5,24,384]{2,1,0:T(8,128)S(1)}, f32[5,24,384]{2,1,0:T(8,128)S(1)}, u32[]{:S(2)}, u32[]{:S(2)}) collective-permute-start(f32[5,24,384]{2,1,0:T(8,128)S(1)} %collective-permute-done.8), channel_id=1, source_target_pairs={{32,60},{33,61},{34,62},{35,63},{36,32},{37,33},{38,34},{39,35},{4... | collective-permute-start | bytes 552968 | tf_op jit(solution)/shard_map/ppermute | solution.py:40
  60.6 1.9 %collective-permute-start.11 = (f32[5,24,384]{2,1,0:T(8,128)S(1)}, f32[5,24,384]{2,1,0:T(8,128)S(1)}, u32[]{:S(2)}, u32[]{:S(2)}) collective-permute-start(f32[5,24,384]{2,1,0:T(8,128)S(1)} %collective-permute-done.9), channel_id=1, source_target_pairs={{32,36},{33,37},{34,38},{35,39},{36,40},{37,41},{38,42},{39,43},{4... | collective-permute-start | bytes 552968 | tf_op jit(solution)/shard_map/ppermute | solution.py:40
  62.5 0.8 fusion.table_ref
  63.3 5.2 %localize.1.local_ref = bf16[4,512,384]{2,1,0:T(8,128)(2,1)} custom-call(s32[48]{0:T(128)} %reshape.26.mask_ref, bf16[4,512,384]{2,1,0:T(8,128)(2,1)} %taper_ref.1, bf16[384,384]{1,0:T(8,128)(2,1)} %fusion.table_ref), custom_call_target="tpu_custom_call" | custom-call | flops 603979776 | bytes 4194304 | tf_op jit(solution)/shard_map/localize/pallas_call | solution.py:193
  68.7 2.3 %collective-permute-start.12 = (f32[4,5,24,384]{3,2,1,0:T(8,128)S(1)}, f32[4,5,24,384]{3,2,1,0:T(8,128)S(1)}, u32[]{:S(2)}, u32[]{:S(2)}) collective-permute-start(f32[4,5,24,384]{3,2,1,0:T(8,128)S(1)} %get-tuple-element.19), channel_id=1, source_target_pairs={{0,4},{1,5},{2,6},{3,7},{4,8},{5,9},{6,10},{7,11},{8,12},{9,13},{1... | collective-permute-start | bytes 2211848 | tf_op jit(solution)/shard_map/ppermute | solution.py:40
  71.0 4.4 %collective-permute-start.13 = (f32[4,5,24,384]{3,2,1,0:T(8,128)S(1)}, f32[4,5,24,384]{3,2,1,0:T(8,128)S(1)}, u32[]{:S(2)}, u32[]{:S(2)}) collective-permute-start(f32[4,5,24,384]{3,2,1,0:T(8,128)S(1)} %get-tuple-element.29), channel_id=1, source_target_pairs={{0,28},{1,29},{2,30},{3,31},{4,0},{5,1},{6,2},{7,3},{8,4},{9,5},{1... | collective-permute-start | bytes 2211848 | tf_op jit(solution)/shard_map/ppermute | solution.py:40
  75.4 6.9 %collective-permute-done.12.refs_3_ = f32[4,5,24,384]{3,2,1,0:T(8,128)S(1)} collective-permute-done((f32[4,5,24,384]{3,2,1,0:T(8,128)S(1)}, f32[4,5,24,384]{3,2,1,0:T(8,128)S(1)}, u32[]{:S(2)}, u32[]{:S(2)}) %collective-permute-start.12) | collective-permute-done | bytes 737312 | tf_op jit(solution)/shard_map/ppermute | solution.py:40
  82.4 1.9 %collective-permute-start.14 = (f32[4,5,24,384]{3,2,1,0:T(8,128)S(1)}, f32[4,5,24,384]{3,2,1,0:T(8,128)S(1)}, u32[]{:S(2)}, u32[]{:S(2)}) collective-permute-start(f32[4,5,24,384]{3,2,1,0:T(8,128)S(1)} %broadcast_select_fusion), channel_id=1, source_target_pairs={{0,4},{1,5},{2,6},{3,7},{4,8},{5,9},{6,10},{7,11},{8,12},{9,13},{1... | collective-permute-start | bytes 2211848 | tf_op jit(solution)/shard_map/ppermute | solution.py:40
  84.3 4.6 %collective-permute-start.15 = (f32[4,5,24,384]{3,2,1,0:T(8,128)S(1)}, f32[4,5,24,384]{3,2,1,0:T(8,128)S(1)}, u32[]{:S(2)}, u32[]{:S(2)}) collective-permute-start(f32[4,5,24,384]{3,2,1,0:T(8,128)S(1)} %collective-permute-done.13.refs_4_), channel_id=1, source_target_pairs={{0,28},{1,29},{2,30},{3,31},{4,0},{5,1},{6,2},{7,3},{8,4},{9,5},{1... | collective-permute-start | bytes 2211848 | tf_op jit(solution)/shard_map/ppermute | solution.py:40
  88.9 2.2 %collective-permute-start.18 = (f32[4,5,24,384]{3,2,1,0:T(8,128)S(1)}, f32[4,5,24,384]{3,2,1,0:T(8,128)S(1)}, u32[]{:S(2)}, u32[]{:S(2)}) collective-permute-start(f32[4,5,24,384]{3,2,1,0:T(8,128)S(1)} %copy-done.5), channel_id=1, source_target_pairs={{0,32},{1,33},{2,34},{3,35},{4,36},{5,37},{6,38},{7,39},{8,40},{9,... | collective-permute-start | bytes 2211848 | tf_op jit(solution)/shard_map/ppermute | solution.py:40
  91.1 2.2 %collective-permute-start.19 = (f32[4,5,24,384]{3,2,1,0:T(8,128)S(1)}, f32[4,5,24,384]{3,2,1,0:T(8,128)S(1)}, u32[]{:S(2)}, u32[]{:S(2)}) collective-permute-start(f32[4,5,24,384]{3,2,1,0:T(8,128)S(1)} %collective-permute-done.6.refs_1_), channel_id=1, source_target_pairs={{0,32},{1,33},{2,34},{3,35},{4,36},{5,37},{6,38},{7,39},{8,40},{9,... | collective-permute-start | bytes 2211848 | tf_op jit(solution)/shard_map/ppermute | solution.py:40
  93.3 2.2 %collective-permute-start.20 = (f32[4,5,24,384]{3,2,1,0:T(8,128)S(1)}, f32[4,5,24,384]{3,2,1,0:T(8,128)S(1)}, u32[]{:S(2)}, u32[]{:S(2)}) collective-permute-start(f32[4,5,24,384]{3,2,1,0:T(8,128)S(1)} %collective-permute-done.7.refs_2_), channel_id=1, source_target_pairs={{0,32},{1,33},{2,34},{3,35},{4,36},{5,37},{6,38},{7,39},{8,40},{9,... | collective-permute-start | bytes 2211848 | tf_op jit(solution)/shard_map/ppermute | solution.py:40
  95.4 0.6 collective-permute-done.14.refs_5_
  96.1 2.5 %collective-permute-start.27 = (f32[4,5,24,384]{3,2,1,0:T(8,128)S(1)}, f32[4,5,24,384]{3,2,1,0:T(8,128)S(1)}, u32[]{:S(2)}, u32[]{:S(2)}) collective-permute-start(f32[4,5,24,384]{3,2,1,0:T(8,128)S(1)} %get-tuple-element.26.refs_9_), channel_id=1, source_target_pairs={{32,0},{33,1},{34,2},{35,3},{36,4},{37,5},{38,6},{39,7},{40,8},{41... | collective-permute-start | bytes 2211848 | tf_op jit(solution)/shard_map/ppermute | solution.py:40
  98.6 0.7 collective-permute-start.16
  99.4 0.7 collective-permute-start.17
  100.1 7.5 %collective-permute-start.21 = (f32[4,5,24,384]{3,2,1,0:T(8,128)S(1)}, f32[4,5,24,384]{3,2,1,0:T(8,128)S(1)}, u32[]{:S(2)}, u32[]{:S(2)}) collective-permute-start(f32[4,5,24,384]{3,2,1,0:T(8,128)S(1)} %collective-permute-done.12.refs_3_), channel_id=1, source_target_pairs={{0,32},{1,33},{2,34},{3,35},{4,36},{5,37},{6,38},{7,39},{8,40},{9,... | collective-permute-start | bytes 2211848 | tf_op jit(solution)/shard_map/ppermute | solution.py:40
  107.7 1.9 %collective-permute-start.22 = (f32[4,5,24,384]{3,2,1,0:T(8,128)S(1)}, f32[4,5,24,384]{3,2,1,0:T(8,128)S(1)}, u32[]{:S(2)}, u32[]{:S(2)}) collective-permute-start(f32[4,5,24,384]{3,2,1,0:T(8,128)S(1)} %collective-permute-done.13.refs_4_), channel_id=1, source_target_pairs={{0,32},{1,33},{2,34},{3,35},{4,36},{5,37},{6,38},{7,39},{8,40},{9,... | collective-permute-start | bytes 2211848 | tf_op jit(solution)/shard_map/ppermute | solution.py:40
  109.6 1.3 collective-permute-start.25
  110.9 3.1 %collective-permute-start.23 = (f32[4,5,24,384]{3,2,1,0:T(8,128)S(1)}, f32[4,5,24,384]{3,2,1,0:T(8,128)S(1)}, u32[]{:S(2)}, u32[]{:S(2)}) collective-permute-start(f32[4,5,24,384]{3,2,1,0:T(8,128)S(1)} %collective-permute-done.14.refs_5_), channel_id=1, source_target_pairs={{0,32},{1,33},{2,34},{3,35},{4,36},{5,37},{6,38},{7,39},{8,40},{9,... | collective-permute-start | bytes 2211848 | tf_op jit(solution)/shard_map/ppermute | solution.py:40
  114.0 1.9 %collective-permute-start.24 = (f32[4,5,24,384]{3,2,1,0:T(8,128)S(1)}, f32[4,5,24,384]{3,2,1,0:T(8,128)}, u32[]{:S(2)}, u32[]{:S(2)}) collective-permute-start(f32[4,5,24,384]{3,2,1,0:T(8,128)S(1)} %collective-permute-done.15.refs_6_), channel_id=1, source_target_pairs={{0,32},{1,33},{2,34},{3,35},{4,36},{5,37},{6,38},{7,39},{8,40},{9,... | collective-permute-start | bytes 2211848 | tf_op jit(solution)/shard_map/ppermute | solution.py:40
  116.0 1.3 collective-permute-start.26
  117.3 2.2 %collective-permute-done.26.refs_18_ = f32[2,5,24,384]{3,2,1,0:T(8,128)S(1)} collective-permute-done((f32[2,5,24,384]{3,2,1,0:T(8,128)S(1)}, f32[2,5,24,384]{3,2,1,0:T(8,128)S(1)}, u32[]{:S(2)}, u32[]{:S(2)}) %collective-permute-start.26) | collective-permute-done | bytes 368672 | tf_op jit(solution)/shard_map/ppermute | solution.py:40
  119.6 0.7 copy-done.23
  120.3 0.9 copy-done.19
  121.2 20.1 %ticks.1 = f32[512,768]{1,0:T(8,128)} custom-call(s32[1]{0:T(128)} %bitcast.core_ref.where_ref, f32[512,768]{1,0:T(8,128)} %state_ref.1, bf16[4,512,384]{2,1,0:T(8,128)(2,1)} %localize.1.local_ref, f32[4,5,24,384]{3,2,1,0:T(8,128)} %copy-done.4, f32[4,5,24,384]{3,2,1,0:T(8,128)} %copy-done, f32[4,5,24,384]{3,2,1,0:T(8,128)} %copy-done.1, ...), custom_call_target="tpu_custom_call" | custom-call | flops 7247757312 | bytes 16777216 | tf_op jit(solution)/shard_map/ticks/pallas_call | solution.py:286
  (77 shorter events, 2.0 us)
Async XLA Ops:
  0.0 53.8 %copy-start.11 = (s32[4,4,3]{1,0,2:T(4,128)S(1)}, s32[4,4,3]{1,0,2:T(4,128)}, u32[]{:S(2)}) copy-start(s32[4,4,3]{1,0,2:T(4,128)} %param.10) | copy-start | bytes 580
  1.7 9.8 %collective-permute-start = (f32[24,384]{1,0:T(8,128)}, f32[24,384]{1,0:T(8,128)S(1)}, u32[]{:S(2)}, u32[]{:S(2)}) collective-permute-start(f32[24,384]{1,0:T(8,128)} %get-tuple-element.17), channel_id=1, source_target_pairs={{0,32},{1,33},{2,34},{3,35},{4,36},{5,37},{6,38},{7,39},{8,40},{9,... | collective-permute-start | bytes 110600 | tf_op jit(solution)/shard_map/ppermute | solution.py:40
  13.6 4.4 %collective-permute-start.1 = (f32[2,24,384]{2,1,0:T(8,128)}, f32[2,24,384]{2,1,0:T(8,128)S(1)}, u32[]{:S(2)}, u32[]{:S(2)}) collective-permute-start(f32[2,24,384]{2,1,0:T(8,128)} %pair.1.pair_ref), channel_id=1, source_target_pairs={{0,64},{1,65},{2,66},{3,67},{4,68},{5,69},{6,70},{7,71},{8,72},{9,... | collective-permute-start | bytes 221192 | tf_op jit(solution)/shard_map/ppermute | solution.py:40
  15.6 2.3 %collective-permute-start.2 = (f32[24,384]{1,0:T(8,128)S(1)}, f32[24,384]{1,0:T(8,128)S(1)}, u32[]{:S(2)}, u32[]{:S(2)}) collective-permute-start(f32[24,384]{1,0:T(8,128)S(1)} %slice_bitcast_fusion), channel_id=1, source_target_pairs={{0,128},{1,129},{2,130},{3,131},{4,132},{5,133},{6,134},{7,135},{8... | collective-permute-start | bytes 110600 | tf_op jit(solution)/shard_map/ppermute | solution.py:40
  20.3 13.3 %collective-permute-start.3 = (f32[5,24,384]{2,1,0:T(8,128)}, f32[5,24,384]{2,1,0:T(8,128)S(1)}, u32[]{:S(2)}, u32[]{:S(2)}) collective-permute-start(f32[5,24,384]{2,1,0:T(8,128)} %share.1), channel_id=1, source_target_pairs={{0,1},{1,2},{2,3},{3,0},{4,5},{5,6},{6,7},{7,4},{8,9},{9,10},{10,1... | collective-permute-start | bytes 552968 | tf_op jit(solution)/shard_map/ppermute | solution.py:40
  23.8 12.4 %collective-permute-start.4 = (f32[5,24,384]{2,1,0:T(8,128)}, f32[5,24,384]{2,1,0:T(8,128)S(1)}, u32[]{:S(2)}, u32[]{:S(2)}) collective-permute-start(f32[5,24,384]{2,1,0:T(8,128)} %share.1), channel_id=1, source_target_pairs={{0,3},{1,0},{2,1},{3,2},{4,7},{5,4},{6,5},{7,6},{8,11},{9,8},{10,9... | collective-permute-start | bytes 552968 | tf_op jit(solution)/shard_map/ppermute | solution.py:40
  33.6 7.5 %collective-permute-start.5 = (f32[5,24,384]{2,1,0:T(8,128)S(1)}, f32[5,24,384]{2,1,0:T(8,128)S(1)}, u32[]{:S(2)}, u32[]{:S(2)}) collective-permute-start(f32[5,24,384]{2,1,0:T(8,128)S(1)} %collective-permute-done.3), channel_id=1, source_target_pairs={{0,1},{1,2},{2,3},{3,0},{4,5},{5,6},{6,7},{7,4},{8,9},{9,10},{10,1... | collective-permute-start | bytes 552968 | tf_op jit(solution)/shard_map/ppermute | solution.py:40
  42.0 26.4 %copy-start.4 = (f32[4,5,24,384]{3,2,1,0:T(8,128)}, f32[4,5,24,384]{3,2,1,0:T(8,128)S(1)}, u32[]{:S(2)}) copy-start(f32[4,5,24,384]{3,2,1,0:T(8,128)S(1)} %pad_maximum_fusion.refs_0_) | copy-start | bytes 2211844
  42.0 26.4 %collective-permute-start.7 = (f32[4,5,24,384]{3,2,1,0:T(8,128)S(1)}, f32[4,5,24,384]{3,2,1,0:T(8,128)S(1)}, u32[]{:S(2)}, u32[]{:S(2)}) collective-permute-start(f32[4,5,24,384]{3,2,1,0:T(8,128)S(1)} %pad_maximum_fusion.refs_0_), channel_id=1, source_target_pairs={{0,28},{1,29},{2,30},{3,31},{4,0},{5,1},{6,2},{7,3},{8,4},{9,5},{1... | collective-permute-start | bytes 2211848 | tf_op jit(solution)/shard_map/ppermute | solution.py:40
  46.4 22.0 %collective-permute-start.6 = (f32[4,5,24,384]{3,2,1,0:T(8,128)S(1)}, f32[4,5,24,384]{3,2,1,0:T(8,128)S(1)}, u32[]{:S(2)}, u32[]{:S(2)}) collective-permute-start(f32[4,5,24,384]{3,2,1,0:T(8,128)S(1)} %pad_maximum_fusion.refs_0_), channel_id=1, source_target_pairs={{0,4},{1,5},{2,6},{3,7},{4,8},{5,9},{6,10},{7,11},{8,12},{9,13},{1... | collective-permute-start | bytes 2211848 | tf_op jit(solution)/shard_map/ppermute | solution.py:40
  48.4 6.9 %collective-permute-start.8 = (f32[5,24,384]{2,1,0:T(8,128)S(1)}, f32[5,24,384]{2,1,0:T(8,128)S(1)}, u32[]{:S(2)}, u32[]{:S(2)}) collective-permute-start(f32[5,24,384]{2,1,0:T(8,128)S(1)} %collective-permute-done.4), channel_id=1, source_target_pairs={{32,60},{33,61},{34,62},{35,63},{36,32},{37,33},{38,34},{39,35},{4... | collective-permute-start | bytes 552968 | tf_op jit(solution)/shard_map/ppermute | solution.py:40
  50.8 9.7 %collective-permute-start.9 = (f32[5,24,384]{2,1,0:T(8,128)S(1)}, f32[5,24,384]{2,1,0:T(8,128)S(1)}, u32[]{:S(2)}, u32[]{:S(2)}) collective-permute-start(f32[5,24,384]{2,1,0:T(8,128)S(1)} %collective-permute-done.5), channel_id=1, source_target_pairs={{32,36},{33,37},{34,38},{35,39},{36,40},{37,41},{38,42},{39,43},{4... | collective-permute-start | bytes 552968 | tf_op jit(solution)/shard_map/ppermute | solution.py:40
  55.2 13.2 %collective-permute-start.10 = (f32[5,24,384]{2,1,0:T(8,128)S(1)}, f32[5,24,384]{2,1,0:T(8,128)S(1)}, u32[]{:S(2)}, u32[]{:S(2)}) collective-permute-start(f32[5,24,384]{2,1,0:T(8,128)S(1)} %collective-permute-done.8), channel_id=1, source_target_pairs={{32,60},{33,61},{34,62},{35,63},{36,32},{37,33},{38,34},{39,35},{4... | collective-permute-start | bytes 552968 | tf_op jit(solution)/shard_map/ppermute | solution.py:40
  60.6 7.9 %collective-permute-start.11 = (f32[5,24,384]{2,1,0:T(8,128)S(1)}, f32[5,24,384]{2,1,0:T(8,128)S(1)}, u32[]{:S(2)}, u32[]{:S(2)}) collective-permute-start(f32[5,24,384]{2,1,0:T(8,128)S(1)} %collective-permute-done.9), channel_id=1, source_target_pairs={{32,36},{33,37},{34,38},{35,39},{36,40},{37,41},{38,42},{39,43},{4... | collective-permute-start | bytes 552968 | tf_op jit(solution)/shard_map/ppermute | solution.py:40
  68.5 24.8 %copy-start.1 = (f32[4,5,24,384]{3,2,1,0:T(8,128)}, f32[4,5,24,384]{3,2,1,0:T(8,128)S(1)}, u32[]{:S(2)}) copy-start(f32[4,5,24,384]{3,2,1,0:T(8,128)S(1)} %collective-permute-done.7.refs_2_) | copy-start | bytes 2211844
  68.5 22.6 %copy-start = (f32[4,5,24,384]{3,2,1,0:T(8,128)}, f32[4,5,24,384]{3,2,1,0:T(8,128)S(1)}, u32[]{:S(2)}) copy-start(f32[4,5,24,384]{3,2,1,0:T(8,128)S(1)} %collective-permute-done.6.refs_1_) | copy-start | bytes 2211844
  68.7 30.7 %copy-start.2 = (f32[4,5,24,384]{3,2,1,0:T(8,128)}, f32[4,5,24,384]{3,2,1,0:T(8,128)S(1)}, u32[]{:S(2)}) copy-start(f32[4,5,24,384]{3,2,1,0:T(8,128)S(1)} %get-tuple-element.26.refs_9_) | copy-start | bytes 2211844
  68.7 20.2 %copy-start.5 = (f32[4,5,24,384]{3,2,1,0:T(8,128)S(1)}, f32[4,5,24,384]{3,2,1,0:T(8,128)}, u32[]{:S(2)}) copy-start(f32[4,5,24,384]{3,2,1,0:T(8,128)} %copy-done.4) | copy-start | bytes 2211844
  68.7 13.6 %collective-permute-start.12 = (f32[4,5,24,384]{3,2,1,0:T(8,128)S(1)}, f32[4,5,24,384]{3,2,1,0:T(8,128)S(1)}, u32[]{:S(2)}, u32[]{:S(2)}) collective-permute-start(f32[4,5,24,384]{3,2,1,0:T(8,128)S(1)} %get-tuple-element.19), channel_id=1, source_target_pairs={{0,4},{1,5},{2,6},{3,7},{4,8},{5,9},{6,10},{7,11},{8,12},{9,13},{1... | collective-permute-start | bytes 2211848 | tf_op jit(solution)/shard_map/ppermute | solution.py:40
  71.0 13.3 %collective-permute-start.13 = (f32[4,5,24,384]{3,2,1,0:T(8,128)S(1)}, f32[4,5,24,384]{3,2,1,0:T(8,128)S(1)}, u32[]{:S(2)}, u32[]{:S(2)}) collective-permute-start(f32[4,5,24,384]{3,2,1,0:T(8,128)S(1)} %get-tuple-element.29), channel_id=1, source_target_pairs={{0,28},{1,29},{2,30},{3,31},{4,0},{5,1},{6,2},{7,3},{8,4},{9,5},{1... | collective-permute-start | bytes 2211848 | tf_op jit(solution)/shard_map/ppermute | solution.py:40
  82.3 17.8 %copy-start.3 = (f32[4,5,24,384]{3,2,1,0:T(8,128)}, f32[4,5,24,384]{3,2,1,0:T(8,128)S(1)}, u32[]{:S(2)}) copy-start(f32[4,5,24,384]{3,2,1,0:T(8,128)S(1)} %collective-permute-done.12.refs_3_) | copy-start | bytes 2211844
  82.4 13.7 %collective-permute-start.14 = (f32[4,5,24,384]{3,2,1,0:T(8,128)S(1)}, f32[4,5,24,384]{3,2,1,0:T(8,128)S(1)}, u32[]{:S(2)}, u32[]{:S(2)}) collective-permute-start(f32[4,5,24,384]{3,2,1,0:T(8,128)S(1)} %broadcast_select_fusion), channel_id=1, source_target_pairs={{0,4},{1,5},{2,6},{3,7},{4,8},{5,9},{6,10},{7,11},{8,12},{9,13},{1... | collective-permute-start | bytes 2211848 | tf_op jit(solution)/shard_map/ppermute | solution.py:40
  84.3 35.3 %copy-start.12 = (f32[4,5,24,384]{3,2,1,0:T(8,128)}, f32[4,5,24,384]{3,2,1,0:T(8,128)S(1)}, u32[]{:S(2)}) copy-start(f32[4,5,24,384]{3,2,1,0:T(8,128)S(1)} %collective-permute-done.13.refs_4_) | copy-start | bytes 2211844
  84.3 14.3 %collective-permute-start.15 = (f32[4,5,24,384]{3,2,1,0:T(8,128)S(1)}, f32[4,5,24,384]{3,2,1,0:T(8,128)S(1)}, u32[]{:S(2)}, u32[]{:S(2)}) collective-permute-start(f32[4,5,24,384]{3,2,1,0:T(8,128)S(1)} %collective-permute-done.13.refs_4_), channel_id=1, source_target_pairs={{0,28},{1,29},{2,30},{3,31},{4,0},{5,1},{6,2},{7,3},{8,4},{9,5},{1... | collective-permute-start | bytes 2211848 | tf_op jit(solution)/shard_map/ppermute | solution.py:40
  88.9 10.5 %collective-permute-start.18 = (f32[4,5,24,384]{3,2,1,0:T(8,128)S(1)}, f32[4,5,24,384]{3,2,1,0:T(8,128)S(1)}, u32[]{:S(2)}, u32[]{:S(2)}) collective-permute-start(f32[4,5,24,384]{3,2,1,0:T(8,128)S(1)} %copy-done.5), channel_id=1, source_target_pairs={{0,32},{1,33},{2,34},{3,35},{4,36},{5,37},{6,38},{7,39},{8,40},{9,... | collective-permute-start | bytes 2211848 | tf_op jit(solution)/shard_map/ppermute | solution.py:40
  91.1 9.0 %collective-permute-start.19 = (f32[4,5,24,384]{3,2,1,0:T(8,128)S(1)}, f32[4,5,24,384]{3,2,1,0:T(8,128)S(1)}, u32[]{:S(2)}, u32[]{:S(2)}) collective-permute-start(f32[4,5,24,384]{3,2,1,0:T(8,128)S(1)} %collective-permute-done.6.refs_1_), channel_id=1, source_target_pairs={{0,32},{1,33},{2,34},{3,35},{4,36},{5,37},{6,38},{7,39},{8,40},{9,... | collective-permute-start | bytes 2211848 | tf_op jit(solution)/shard_map/ppermute | solution.py:40
  93.3 14.4 %collective-permute-start.20 = (f32[4,5,24,384]{3,2,1,0:T(8,128)S(1)}, f32[4,5,24,384]{3,2,1,0:T(8,128)S(1)}, u32[]{:S(2)}, u32[]{:S(2)}) collective-permute-start(f32[4,5,24,384]{3,2,1,0:T(8,128)S(1)} %collective-permute-done.7.refs_2_), channel_id=1, source_target_pairs={{0,32},{1,33},{2,34},{3,35},{4,36},{5,37},{6,38},{7,39},{8,40},{9,... | collective-permute-start | bytes 2211848 | tf_op jit(solution)/shard_map/ppermute | solution.py:40
  96.1 25.1 %copy-start.6 = (f32[4,5,24,384]{3,2,1,0:T(8,128)}, f32[4,5,24,384]{3,2,1,0:T(8,128)S(1)}, u32[]{:S(2)}) copy-start(f32[4,5,24,384]{3,2,1,0:T(8,128)S(1)} %collective-permute-done.14.refs_5_) | copy-start | bytes 2211844
  96.1 14.8 %collective-permute-start.27 = (f32[4,5,24,384]{3,2,1,0:T(8,128)S(1)}, f32[4,5,24,384]{3,2,1,0:T(8,128)S(1)}, u32[]{:S(2)}, u32[]{:S(2)}) collective-permute-start(f32[4,5,24,384]{3,2,1,0:T(8,128)S(1)} %get-tuple-element.26.refs_9_), channel_id=1, source_target_pairs={{32,0},{33,1},{34,2},{35,3},{36,4},{37,5},{38,6},{39,7},{40,8},{41... | collective-permute-start | bytes 2211848 | tf_op jit(solution)/shard_map/ppermute | solution.py:40
  98.6 22.6 %copy-start.7 = (f32[4,5,24,384]{3,2,1,0:T(8,128)}, f32[4,5,24,384]{3,2,1,0:T(8,128)S(1)}, u32[]{:S(2)}) copy-start(f32[4,5,24,384]{3,2,1,0:T(8,128)S(1)} %collective-permute-done.15.refs_6_) | copy-start | bytes 2211844
  98.6 11.0 %collective-permute-start.16 = (f32[2,5,24,384]{3,2,1,0:T(8,128)S(1)}, f32[2,5,24,384]{3,2,1,0:T(8,128)S(1)}, u32[]{:S(2)}, u32[]{:S(2)}) collective-permute-start(f32[2,5,24,384]{3,2,1,0:T(8,128)S(1)} %slice.31), channel_id=1, source_target_pairs={{0,4},{1,5},{2,6},{3,7},{4,8},{5,9},{6,10},{7,11},{8,12},{9,13},{1... | collective-permute-start | bytes 1105928 | tf_op jit(solution)/shard_map/ppermute | solution.py:40
  99.4 20.2 %copy-start.13 = (f32[4,5,24,384]{3,2,1,0:T(8,128)}, f32[4,5,24,384]{3,2,1,0:T(8,128)S(1)}, u32[]{:S(2)}) copy-start(f32[4,5,24,384]{3,2,1,0:T(8,128)S(1)} %collective-permute-done.18.refs_10_) | copy-start | bytes 2211844
  99.4 14.6 %collective-permute-start.17 = (f32[2,5,24,384]{3,2,1,0:T(8,128)S(1)}, f32[2,5,24,384]{3,2,1,0:T(8,128)S(1)}, u32[]{:S(2)}, u32[]{:S(2)}) collective-permute-start(f32[2,5,24,384]{3,2,1,0:T(8,128)S(1)} %slice.32), channel_id=1, source_target_pairs={{0,28},{1,29},{2,30},{3,31},{4,0},{5,1},{6,2},{7,3},{8,4},{9,5},{1... | collective-permute-start | bytes 1105928 | tf_op jit(solution)/shard_map/ppermute | solution.py:40
  100.1 19.5 %copy-start.14 = (f32[4,5,24,384]{3,2,1,0:T(8,128)}, f32[4,5,24,384]{3,2,1,0:T(8,128)S(1)}, u32[]{:S(2)}) copy-start(f32[4,5,24,384]{3,2,1,0:T(8,128)S(1)} %collective-permute-done.19.refs_11_) | copy-start | bytes 2211844
  100.1 17.2 %collective-permute-start.21 = (f32[4,5,24,384]{3,2,1,0:T(8,128)S(1)}, f32[4,5,24,384]{3,2,1,0:T(8,128)S(1)}, u32[]{:S(2)}, u32[]{:S(2)}) collective-permute-start(f32[4,5,24,384]{3,2,1,0:T(8,128)S(1)} %collective-permute-done.12.refs_3_), channel_id=1, source_target_pairs={{0,32},{1,33},{2,34},{3,35},{4,36},{5,37},{6,38},{7,39},{8,40},{9,... | collective-permute-start | bytes 2211848 | tf_op jit(solution)/shard_map/ppermute | solution.py:40
  107.6 11.9 %copy-start.15 = (f32[4,5,24,384]{3,2,1,0:T(8,128)}, f32[4,5,24,384]{3,2,1,0:T(8,128)S(1)}, u32[]{:S(2)}) copy-start(f32[4,5,24,384]{3,2,1,0:T(8,128)S(1)} %collective-permute-done.20.refs_12_) | copy-start | bytes 2211844
  107.7 9.6 %collective-permute-start.22 = (f32[4,5,24,384]{3,2,1,0:T(8,128)S(1)}, f32[4,5,24,384]{3,2,1,0:T(8,128)S(1)}, u32[]{:S(2)}, u32[]{:S(2)}) collective-permute-start(f32[4,5,24,384]{3,2,1,0:T(8,128)S(1)} %collective-permute-done.13.refs_4_), channel_id=1, source_target_pairs={{0,32},{1,33},{2,34},{3,35},{4,36},{5,37},{6,38},{7,39},{8,40},{9,... | collective-permute-start | bytes 2211848 | tf_op jit(solution)/shard_map/ppermute | solution.py:40
  109.6 11.6 %copy-start.20 = (f32[2,5,24,384]{3,2,1,0:T(8,128)}, f32[2,5,24,384]{3,2,1,0:T(8,128)S(1)}, u32[]{:S(2)}) copy-start(f32[2,5,24,384]{3,2,1,0:T(8,128)S(1)} %collective-permute-done.16.refs_7_) | copy-start | bytes 1105924
  109.6 6.3 %collective-permute-start.25 = (f32[2,5,24,384]{3,2,1,0:T(8,128)S(1)}, f32[2,5,24,384]{3,2,1,0:T(8,128)S(1)}, u32[]{:S(2)}, u32[]{:S(2)}) collective-permute-start(f32[2,5,24,384]{3,2,1,0:T(8,128)S(1)} %collective-permute-done.16.refs_7_), channel_id=1, source_target_pairs={{0,32},{1,33},{2,34},{3,35},{4,36},{5,37},{6,38},{7,39},{8,40},{9,... | collective-permute-start | bytes 1105928 | tf_op jit(solution)/shard_map/ppermute | solution.py:40
  110.9 8.7 %copy-start.16 = (f32[4,5,24,384]{3,2,1,0:T(8,128)}, f32[4,5,24,384]{3,2,1,0:T(8,128)S(1)}, u32[]{:S(2)}) copy-start(f32[4,5,24,384]{3,2,1,0:T(8,128)S(1)} %collective-permute-done.27.refs_19_) | copy-start | bytes 2211844
  110.9 8.6 %collective-permute-start.23 = (f32[4,5,24,384]{3,2,1,0:T(8,128)S(1)}, f32[4,5,24,384]{3,2,1,0:T(8,128)S(1)}, u32[]{:S(2)}, u32[]{:S(2)}) collective-permute-start(f32[4,5,24,384]{3,2,1,0:T(8,128)S(1)} %collective-permute-done.14.refs_5_), channel_id=1, source_target_pairs={{0,32},{1,33},{2,34},{3,35},{4,36},{5,37},{6,38},{7,39},{8,40},{9,... | collective-permute-start | bytes 2211848 | tf_op jit(solution)/shard_map/ppermute | solution.py:40
  114.0 5.6 %copy-start.21 = (f32[2,5,24,384]{3,2,1,0:T(8,128)}, f32[2,5,24,384]{3,2,1,0:T(8,128)S(1)}, u32[]{:S(2)}) copy-start(f32[2,5,24,384]{3,2,1,0:T(8,128)S(1)} %collective-permute-done.17.refs_8_) | copy-start | bytes 1105924
  114.0 7.2 %collective-permute-start.24 = (f32[4,5,24,384]{3,2,1,0:T(8,128)S(1)}, f32[4,5,24,384]{3,2,1,0:T(8,128)}, u32[]{:S(2)}, u32[]{:S(2)}) collective-permute-start(f32[4,5,24,384]{3,2,1,0:T(8,128)S(1)} %collective-permute-done.15.refs_6_), channel_id=1, source_target_pairs={{0,32},{1,33},{2,34},{3,35},{4,36},{5,37},{6,38},{7,39},{8,40},{9,... | collective-permute-start | bytes 2211848 | tf_op jit(solution)/shard_map/ppermute | solution.py:40
  115.9 3.7 %copy-start.22 = (f32[2,5,24,384]{3,2,1,0:T(8,128)}, f32[2,5,24,384]{3,2,1,0:T(8,128)S(1)}, u32[]{:S(2)}) copy-start(f32[2,5,24,384]{3,2,1,0:T(8,128)S(1)} %collective-permute-done.25.refs_17_) | copy-start | bytes 1105924
  116.0 3.6 %collective-permute-start.26 = (f32[2,5,24,384]{3,2,1,0:T(8,128)S(1)}, f32[2,5,24,384]{3,2,1,0:T(8,128)S(1)}, u32[]{:S(2)}, u32[]{:S(2)}) collective-permute-start(f32[2,5,24,384]{3,2,1,0:T(8,128)S(1)} %collective-permute-done.17.refs_8_), channel_id=1, source_target_pairs={{0,32},{1,33},{2,34},{3,35},{4,36},{5,37},{6,38},{7,39},{8,40},{9,... | collective-permute-start | bytes 1105928 | tf_op jit(solution)/shard_map/ppermute | solution.py:40
  117.3 3.9 %copy-start.17 = (f32[4,5,24,384]{3,2,1,0:T(8,128)}, f32[4,5,24,384]{3,2,1,0:T(8,128)S(1)}, u32[]{:S(2)}) copy-start(f32[4,5,24,384]{3,2,1,0:T(8,128)S(1)} %collective-permute-done.21.refs_13_) | copy-start | bytes 2211844
  117.3 3.9 %copy-start.18 = (f32[4,5,24,384]{3,2,1,0:T(8,128)}, f32[4,5,24,384]{3,2,1,0:T(8,128)S(1)}, u32[]{:S(2)}) copy-start(f32[4,5,24,384]{3,2,1,0:T(8,128)S(1)} %collective-permute-done.22.refs_14_) | copy-start | bytes 2211844
  120.3 0.9 copy-start.19
  (4 other events, 2.6 us)

commit v3 on v2

--- a/solution.py
+++ b/solution.py
@@ -5,6 +5,7 @@
 from jax.experimental import pallas as pl
 from jax.experimental.pallas import tpu as pltpu
 from jax.sharding import PartitionSpec as P
+
 
 MEMBERS = 768
 HALF = 384
@@ -48,8 +49,15 @@
     return lambda y, core, z, x: (y + step, core, z, x) if y + step < N_Y else None
 
 
-def pack_kernel(core_ref, anom_ref, incr_ref, anom_new_ref, incr_new_ref, mine_ref, other_ref, fresh_ref):
+def pack_kernel(core_ref, *refs):
     core = core_ref[0]
+    mine_ref, other_ref, fresh_ref = refs[4:7]
+    copies = [pltpu.make_async_copy(refs[i], refs[7 + i], refs[11].at[i]) for i in range(4)]
+    for copy in copies:
+        copy.start()
+    for copy in copies:
+        copy.wait()
+    anom_ref, incr_ref, anom_new_ref, incr_new_ref = refs[7:11]
     for col in range(HALF // BLOCK):
         to = slice(col * BLOCK, (col + 1) * BLOCK)
         for half, out_ref in ((core, mine_ref), (1 - core, other_ref)):
@@ -66,43 +74,37 @@
         fresh_ref[batch, 20:24] = incr_new_ref[batch, 8:12, mine]
 
 
-def share_kernel(where_ref, pair_ref, below_ref, below2_ref, fresh_ref, out_ref):
-    y = where_ref[0]
-    out_ref[0:2] = pair_ref[...]
-    out_ref[2:4] = jnp.where(y == 0, fresh_ref[0:2], below_ref[...])
-    out_ref[4] = jnp.where(y == 0, fresh_ref[2], jnp.where(y == 1, fresh_ref[0], below2_ref[...]))
-
-
-def pair_kernel(core_ref, mine_ref, other_ref, out_ref):
-    out_ref[1 - core_ref[0]] = mine_ref[...]
-    out_ref[core_ref[0]] = other_ref[...]
-
-
-def small_call(kernel, name, out_shape, scalar, *arrays):
-    vmem = pl.BlockSpec(memory_space=pltpu.VMEM)
-    many = isinstance(out_shape[0], tuple)
-    shapes = tuple(jax.ShapeDtypeStruct(o, F32) for o in (out_shape if many else (out_shape,)))
-    return pl.pallas_call(
-        kernel,
-        out_shape=shapes if many else shapes[0],
-        in_specs=[pl.BlockSpec(memory_space=pltpu.SMEM)] + [vmem] * len(arrays),
-        out_specs=(vmem,) * len(shapes) if many else vmem,
-        name=name,
-    )(scalar.reshape(1), *arrays)
-
-
 def chip_shares(core, y, anom_fly, incr_fly, anom_new, incr_new):
     flat = (SHARE * MEMBERS // BLOCK, BLOCK)
     tile = (PACK, HALF)
-    mine, give, fresh = small_call(
-        pack_kernel, "pack", (tile, tile, (3, *tile)), core,
-        anom_fly.reshape(flat), incr_fly.reshape(flat), anom_new, incr_new,
+    vmem = pl.BlockSpec(memory_space=pltpu.VMEM)
+    mine, give, fresh = pl.pallas_call(
+        pack_kernel,
+        out_shape=tuple(jax.ShapeDtypeStruct(o, F32) for o in (tile, tile, (3, *tile))),
+        in_specs=[pl.BlockSpec(memory_space=pltpu.SMEM)] + [pl.BlockSpec(memory_space=pltpu.HBM)] * 4,
+        out_specs=(vmem, vmem, vmem),
+        scratch_shapes=[pltpu.VMEM(flat, F32)] * 2
+        + [pltpu.VMEM((3, SHARE, MEMBERS), F32)] * 2
+        + [pltpu.SemaphoreType.DMA((4,))],
+        compiler_params=pltpu.CompilerParams(vmem_limit_bytes=4 << 20),
+        name="pack",
+    )(
+        core.reshape(1),
+        *(pltpu.with_memory_space_constraint(a, pltpu.HBM) for a in (anom_fly.reshape(flat), incr_fly.reshape(flat), anom_new, incr_new)),
     )
     other = send(give, flip)
-    pair = small_call(pair_kernel, "pair", (2, *tile), core, mine, other)
+    pair = jnp.stack([jnp.where(core == 1, mine, other), jnp.where(core == 1, other, mine)])
     below = send(pair, up_y(1))
     below2 = send(pair[0], up_y(2))
-    return small_call(share_kernel, "share", (5, *tile), y, pair, below, below2, fresh)
+    return jnp.stack(
+        [
+            pair[0],
+            pair[1],
+            jnp.where(y == 0, fresh[0], below[0]),
+            jnp.where(y == 0, fresh[1], below[1]),
+            jnp.where(y == 0, fresh[2], jnp.where(y == 1, fresh[0], below2)),
+        ]
+    )
 
 
 FAR_Z = (0, 1, -1, 2, -2, 3, -3, 4)
@@ -129,42 +131,44 @@
     return move
 
 
-def hold(value, *others):
-    return lax.optimization_barrier((value, *others))[0]
-
-
-def gather_pieces(core, share, local):
+def gather_pieces(core, share, make_local):
     first = core == 0
     up, down = both((1, 0), (0, 1)), both((-1, 0), (0, -1))
     near_up, near_down = both((0, 1), (1, 0)), both((0, -1), (-1, 0))
     to_second = lambda y, core, z, x: (y, 1, z, x) if core == 0 else None
     to_first = lambda y, core, z, x: (y, 0, z, x) if core == 1 else None
+    only_up, only_down = both(None, (1, 0)), both(None, (-1, 0))
     n1 = send(share, near_up)
+    n3 = send(share, both((0, 2), (2, 0)))
     n2 = send(share, near_down)
-    n3 = send(n1, near_up)
     low = jnp.stack([share, n1, n2, n3])
     up1 = send(low, up)
     down1 = send(low, down)
-    only_up, only_down = both(None, (1, 0)), both(None, (-1, 0))
     n4 = send(n2, only_down)
     n5 = send(n3, only_up)
     n6 = send(n4, only_down)
     n7 = send(n5, only_up)
     high = jnp.stack([n4, n5, n6, n7])
-    up2 = send(hold(jnp.where(first, up1, high), local), up)
+    up2 = send(jnp.where(first, up1, high), up)
     down2 = send(jnp.where(first, down1, high), down)
+    par_low = send(low, flip)
+    par_up1 = send(up1, flip)
+    par_down1 = send(down1, flip)
+    local = make_local(high)
     up3 = send(jnp.where(first, up2, up1), up)
     down3 = send(down2, down)
-    par_low, par_up1, par_down1 = (send(hold(block, up2), flip) for block in (low, up1, down1))
-    par_high = send(hold(high, up2), to_first)
+    par_high = send(high, to_first)
+    par_up2 = send(up2, flip)
+    par_down2 = send(down2, flip)
     far_up = send(up3[:2], both((1, 0), None))
     far_down = send(down3[2:], both((-1, 0), None))
-    par_up2, par_down2 = send(hold(up2, up3), flip), send(hold(down2, up3), flip)
-    par_up3, par_down3 = send(hold(up3, down3), flip), send(down3, flip)
-    par_far_up, par_far_down = send(far_up, to_second), send(far_down, to_second)
+    par_up3 = send(up3, flip)
+    par_down3 = send(down3, flip)
+    par_far_up = send(far_up, to_second)
+    par_far_down = send(far_down, to_second)
     own = [low, up1, down1, up2, down2, up3, down3, far_up, far_down, high]
     par = [par_low, par_up1, par_down1, par_up2, par_down2, par_up3, par_down3, par_far_up, par_far_down, par_high]
-    return own, par
+    return own, par, local
 
 
 def slot_table(core, z, x):
@@ -182,9 +186,9 @@
         rows = pl.ds(rb * BLOCK, BLOCK)
         parts = []
         for ob in range(OBS // BLOCK):
-            flag = mask_ref[(tick * (ROWS // BLOCK) + rb) * (OBS // BLOCK) + ob].astype(F32)
-            tile = taper_ref[0, rows, pl.ds(ob * BLOCK, BLOCK)].astype(F32)
-            parts.append((tile * flag).astype(BF16))
+            flag = mask_ref[(tick * (ROWS // BLOCK) + rb) * (OBS // BLOCK) + ob].astype(F32).astype(BF16)
+            tile = taper_ref[0, rows, pl.ds(ob * BLOCK, BLOCK)]
+            parts.append(tile * flag)
         kept = jnp.concatenate(parts, axis=1)
         out_ref[0, rows, :] = jnp.dot(kept, table_ref[...], preferred_element_type=F32).astype(BF16)
 
@@ -203,6 +207,7 @@
             out_specs=pl.BlockSpec((1, ROWS, SLOTS), lambda t, m: (t, 0, 0)),
         ),
         cost_estimate=pl.CostEstimate(flops=8 * ROWS * OBS * SLOTS, bytes_accessed=4 << 20, transcendentals=0),
+        compiler_params=pltpu.CompilerParams(vmem_limit_bytes=8 << 20),
         name="localize",
     )(block_mask.reshape(-1), taper, table)
 
@@ -212,18 +217,9 @@
     return hi, (a - hi.astype(F32)).astype(BF16)
 
 
-def dot3(a, b, dims):
-    def one(p, q):
-        return lax.dot_general(p, q, (dims, ((), ())), preferred_element_type=F32)
-
-    return one(a[0], b[0]) + one(a[0], b[1]) + one(a[1], b[0])
-
-
 def ticks_kernel(where_ref, state_ref, local_ref, *refs):
-    own_refs, par_refs, out_ref, own_rows, par_rows = refs[:10], refs[10:20], refs[20], refs[21:25], refs[25:29]
+    own_refs, par_refs, out_ref, y_rows, d_rows = refs[:10], refs[10:20], refs[20], refs[21], refs[22]
     core = where_ref[0]
-    mine = pl.ds(pl.multiple_of(core * HALF, BLOCK), HALF)
-    other = pl.ds(pl.multiple_of((1 - core) * HALF, BLOCK), HALF)
 
     @pl.when(pl.program_id(0) == 0)
     def _():
@@ -235,9 +231,13 @@
             return held[7 + part // 2][part % 2, 0]
         return held[9 if array == 1 else max(array - 1, 0)][part, 0]
 
-    def put(rows, at, anom, incr):
-        for (hi, lo), value in ((rows[:2], anom), (rows[2:], incr)):
-            hi[at : at + 16], lo[at : at + 16] = halves(value)
+    def put(columns, at, anom, incr):
+        hi, lo = halves(anom)
+        for part, value in enumerate((hi, lo, hi)):
+            y_rows[at : at + 16, part * MEMBERS + columns : part * MEMBERS + columns + HALF] = value
+        hi, lo = halves(incr)
+        for part, value in enumerate((hi, lo, hi)):
+            d_rows[part * OBS + at : part * OBS + at + 16, columns : columns + HALF] = value
 
     upper = lax.broadcasted_iota(jnp.int32, (8, HALF), 0) < 4
 
@@ -265,18 +265,18 @@
 
         @pl.when(core == me)
         def _(me=me):
-            arrange(own_rows, lambda at: [piece(own_refs, at + k, me == 0) for k in range(4)])
-            arrange(par_rows, lambda at: [piece(par_refs, PARTNER[me][at + k], me == 1) for k in range(4)])
-
-    def both_parts(rows, first):
-        return rows[first][...], rows[first + 1][...]
-
-    trans, plain = ((1,), (1,)), ((1,), (0,))
-    left, right = out_ref[:, mine], out_ref[:, other]
-    cross = dot3(halves(left), both_parts(own_rows, 0), trans) + dot3(halves(right), both_parts(par_rows, 0), trans)
-    weight = halves(local_ref[0].astype(F32) * cross * (1.0 / (MEMBERS - 1)))
-    out_ref[:, mine] = left + dot3(weight, both_parts(own_rows, 2), plain)
-    out_ref[:, other] = right + dot3(weight, both_parts(par_rows, 2), plain)
+            arrange(me * HALF, lambda at: [piece(own_refs, at + k, me == 0) for k in range(4)])
+            arrange((1 - me) * HALF, lambda at: [piece(par_refs, PARTNER[me][at + k], me == 1) for k in range(4)])
+
+    def product(a, b, dims):
+        hi, lo = halves(a)
+        return lax.dot_general(
+            jnp.concatenate([hi, hi, lo], axis=1), b[...], (dims, ((), ())), preferred_element_type=F32
+        )
+
+    cross = product(out_ref[...], y_rows, ((1,), (1,)))
+    weight = local_ref[0].astype(F32) * cross * (1.0 / (MEMBERS - 1))
+    out_ref[...] += product(weight, d_rows, ((1,), (0,)))
 
 
 def run_ticks(core, state, local, own, par):
@@ -295,9 +295,10 @@
             ]
             + ([four] * 7 + [two] * 2 + [four]) * 2,
             out_specs=pl.BlockSpec((ROWS, MEMBERS), lambda t, w: (0, 0)),
-            scratch_shapes=[pltpu.VMEM((OBS, HALF), BF16)] * 8,
+            scratch_shapes=[pltpu.VMEM((OBS, 3 * MEMBERS), BF16), pltpu.VMEM((3 * OBS, MEMBERS), BF16)],
         ),
         cost_estimate=pl.CostEstimate(flops=48 * ROWS * SLOTS * MEMBERS, bytes_accessed=16 << 20, transcendentals=0),
+        compiler_params=pltpu.CompilerParams(vmem_limit_bytes=28 << 20),
         name="ticks",
     )(core.reshape(1), state, local, *own, *par)
 
@@ -306,8 +307,13 @@
     region, place = lax.axis_index("region"), lax.axis_index("var")
     core, y = region % 2, region // 2
     share = chip_shares(core, y, anom_fly, incr_fly, anom_new, incr_new)
-    local = localizers(taper, block_mask, slot_table(core, place // 4, place % 4))
-    own, par = gather_pieces(core, share, local)
+    table = slot_table(core, place // 4, place % 4)
+
+    def make_local(after):
+        held_taper, held_mask, held_table, _ = lax.optimization_barrier((taper, block_mask, table, after))
+        return localizers(held_taper, held_mask, held_table)
+
+    own, par, local = gather_pieces(core, share, make_local)
     return run_ticks(core, state, local, own, par)
 
 
@@ -321,6 +327,5 @@
         P(None, "var", None),
         P(None, "var", None),
     )
-    return jax.shard_map(
-        on_device, mesh=mesh, in_specs=in_specs, out_specs=P(("region", "var"), None), check_vma=False
-    )
+
+    return jax.shard_map(on_device, mesh=mesh, in_specs=in_specs, out_specs=P(("region", "var"), None), check_vma=False)

time: 143 us -> 137 us (0.958)
  the two profiles are of different devices: /device:TPU:1 before, /device:TPU:24 now
where the time goes in v3:
time: 137 us; the launch traced here: 136 us
  starting transfers between devices  75.3 us (55%)
  waiting for transfers between devices  34.2 us (25%)
  Pallas kernels  21.2 us (15%)
  local copies, waits for them, and re-layouts  3.29 us (2%)
  other arithmetic  1.39 us (1%)
    ppermute x28, starting transfers between devices, send(): return lax.ppermute(block, ('region', 'var'), route(move))  75.3 us
    ppermute x28, waiting for transfers between devices, send(): return lax.ppermute(block, ('region', 'var'), route(move))  34.2 us
    pallas_call x1, Pallas kernels, run_ticks(): pl.pallas_call(ticks_kernel, out_shape=jax.ShapeDtypeStruct((ROWS, MEMBER...  17.9 us
  transfers between devices with their start and end apart: 28, of which 11 were waited for; matrix products, arithmetic and copies ran while one was open for 3% of the time, Pallas kernels for 2%

profile of v3, /device:TPU:24, one launch (start us, length us, event | category | flops | bytes accessed | tf_op | source)
XLA Modules:
  0.0 136.0 jit_solution(7818298696640963960)
XLA Ops:
  0.0 1.1 pack.1
  1.1 1.9 %collective-permute-start = (f32[24,384]{1,0:T(8,128)S(1)}, f32[24,384]{1,0:T(8,128)S(1)}, u32[]{:S(2)}, u32[]{:S(2)}) collective-permute-start(f32[24,384]{1,0:T(8,128)S(1)} %get-tuple-element.12), channel_id=1, source_target_pairs={{0,32},{1,33},{2,34},{3,35},{4,36},{5,37},{6,38},{7,39},{8,40},{9,... | collective-permute-start | bytes 110600 | tf_op jit(solution)/shard_map/ppermute | solution.py:41
  3.0 1.2 collective-permute-done
  4.2 4.7 %collective-permute-start.1 = (f32[2,24,384]{2,1,0:T(8,128)S(1)}, f32[2,24,384]{2,1,0:T(8,128)S(1)}, u32[]{:S(2)}, u32[]{:S(2)}) collective-permute-start(f32[2,24,384]{2,1,0:T(8,128)S(1)} %pad_maximum_fusion.2), channel_id=1, source_target_pairs={{0,64},{1,65},{2,66},{3,67},{4,68},{5,69},{6,70},{7,71},{8,72},{9,... | collective-permute-start | bytes 221192 | tf_op jit(solution)/shard_map/ppermute | solution.py:41
  9.0 2.7 %collective-permute-start.2 = (f32[24,384]{1,0:T(8,128)S(1)}, f32[24,384]{1,0:T(8,128)S(1)}, u32[]{:S(2)}, u32[]{:S(2)}) collective-permute-start(f32[24,384]{1,0:T(8,128)S(1)} %get-tuple-element.20), channel_id=1, source_target_pairs={{0,128},{1,129},{2,130},{3,131},{4,132},{5,133},{6,134},{7,135},{8... | collective-permute-start | bytes 110600 | tf_op jit(solution)/shard_map/ppermute | solution.py:41
  11.7 4.0 %collective-permute-done.2 = f32[24,384]{1,0:T(8,128)S(1)} collective-permute-done((f32[24,384]{1,0:T(8,128)S(1)}, f32[24,384]{1,0:T(8,128)S(1)}, u32[]{:S(2)}, u32[]{:S(2)}) %collective-permute-start.2) | collective-permute-done | bytes 36896 | tf_op jit(solution)/shard_map/ppermute | solution.py:41
  15.7 3.4 %collective-permute-start.9 = (f32[5,24,384]{2,1,0:T(8,128)S(1)}, f32[5,24,384]{2,1,0:T(8,128)S(1)}, u32[]{:S(2)}, u32[]{:S(2)}) collective-permute-start(f32[5,24,384]{2,1,0:T(8,128)S(1)} %bitcast_dynamic-update-slice_fusion), channel_id=1, source_target_pairs={{0,1},{1,2},{2,3},{3,0},{4,5},{5,6},{6,7},{7,4},{8,9},{9,10},{10,1... | collective-permute-start | bytes 552968 | tf_op jit(solution)/shard_map/ppermute | solution.py:41
  19.1 4.6 %collective-permute-start.5 = (f32[5,24,384]{2,1,0:T(8,128)S(1)}, f32[5,24,384]{2,1,0:T(8,128)S(1)}, u32[]{:S(2)}, u32[]{:S(2)}) collective-permute-start(f32[5,24,384]{2,1,0:T(8,128)S(1)} %bitcast_dynamic-update-slice_fusion), channel_id=1, source_target_pairs={{0,2},{1,3},{2,0},{3,1},{4,6},{5,7},{6,4},{7,5},{8,10},{9,11},{10,... | collective-permute-start | bytes 552968 | tf_op jit(solution)/shard_map/ppermute | solution.py:41
  23.8 3.3 %collective-permute-start.3 = (f32[5,24,384]{2,1,0:T(8,128)S(1)}, f32[5,24,384]{2,1,0:T(8,128)S(1)}, u32[]{:S(2)}, u32[]{:S(2)}) collective-permute-start(f32[5,24,384]{2,1,0:T(8,128)S(1)} %bitcast_dynamic-update-slice_fusion), channel_id=1, source_target_pairs={{0,3},{1,0},{2,1},{3,2},{4,7},{5,4},{6,5},{7,6},{8,11},{9,8},{10,9... | collective-permute-start | bytes 552968 | tf_op jit(solution)/shard_map/ppermute | solution.py:41
  27.1 0.9 collective-permute-done.5
  28.1 3.1 %collective-permute-done.3 = f32[5,24,384]{2,1,0:T(8,128)S(1)} collective-permute-done((f32[5,24,384]{2,1,0:T(8,128)S(1)}, f32[5,24,384]{2,1,0:T(8,128)S(1)}, u32[]{:S(2)}, u32[]{:S(2)}) %collective-permute-start.3) | collective-permute-done | bytes 184352 | tf_op jit(solution)/shard_map/ppermute | solution.py:41
  31.3 11.3 %collective-permute-start.11 = (f32[4,5,24,384]{3,2,1,0:T(8,128)S(1)}, f32[4,5,24,384]{3,2,1,0:T(8,128)S(1)}, u32[]{:S(2)}, u32[]{:S(2)}) collective-permute-start(f32[4,5,24,384]{3,2,1,0:T(8,128)S(1)} %pad_maximum_fusion.1.refs_0_), channel_id=1, source_target_pairs={{0,28},{1,29},{2,30},{3,31},{4,0},{5,1},{6,2},{7,3},{8,4},{9,5},{1... | collective-permute-start | bytes 2211848 | tf_op jit(solution)/shard_map/ppermute | solution.py:41
  42.6 1.9 %collective-permute-start.10 = (f32[4,5,24,384]{3,2,1,0:T(8,128)S(1)}, f32[4,5,24,384]{3,2,1,0:T(8,128)S(1)}, u32[]{:S(2)}, u32[]{:S(2)}) collective-permute-start(f32[4,5,24,384]{3,2,1,0:T(8,128)S(1)} %pad_maximum_fusion.1.refs_0_), channel_id=1, source_target_pairs={{0,4},{1,5},{2,6},{3,7},{4,8},{5,9},{6,10},{7,11},{8,12},{9,13},{1... | collective-permute-start | bytes 2211848 | tf_op jit(solution)/shard_map/ppermute | solution.py:41
  44.5 0.7 collective-permute-start.6
  45.2 0.7 collective-permute-start.4
  45.9 0.7 collective-permute-start.8
  46.6 0.7 collective-permute-start.7
  47.3 6.2 %collective-permute-done.11.refs_2_ = f32[4,5,24,384]{3,2,1,0:T(8,128)S(1)} collective-permute-done((f32[4,5,24,384]{3,2,1,0:T(8,128)S(1)}, f32[4,5,24,384]{3,2,1,0:T(8,128)S(1)}, u32[]{:S(2)}, u32[]{:S(2)}) %collective-permute-start.11) | collective-permute-done | bytes 737312 | tf_op jit(solution)/shard_map/ppermute | solution.py:41
  53.5 5.6 %collective-permute-done.10.refs_1_ = f32[4,5,24,384]{3,2,1,0:T(8,128)S(1)} collective-permute-done((f32[4,5,24,384]{3,2,1,0:T(8,128)S(1)}, f32[4,5,24,384]{3,2,1,0:T(8,128)S(1)}, u32[]{:S(2)}, u32[]{:S(2)}) %collective-permute-start.10) | collective-permute-done | bytes 737312 | tf_op jit(solution)/shard_map/ppermute | solution.py:41
  59.1 1.0 broadcast_select_fusion.1
  60.2 2.0 %collective-permute-start.13 = (f32[4,5,24,384]{3,2,1,0:T(8,128)S(1)}, f32[4,5,24,384]{3,2,1,0:T(8,128)}, u32[]{:S(2)}, u32[]{:S(2)}) collective-permute-start(f32[4,5,24,384]{3,2,1,0:T(8,128)S(1)} %get-tuple-element.21), channel_id=1, source_target_pairs={{0,28},{1,29},{2,30},{3,31},{4,0},{5,1},{6,2},{7,3},{8,4},{9,5},{1... | collective-permute-start | bytes 2211848 | tf_op jit(solution)/shard_map/ppermute | solution.py:41
  62.3 4.1 %collective-permute-start.12 = (f32[4,5,24,384]{3,2,1,0:T(8,128)S(1)}, f32[4,5,24,384]{3,2,1,0:T(8,128)S(1)}, u32[]{:S(2)}, u32[]{:S(2)}) collective-permute-start(f32[4,5,24,384]{3,2,1,0:T(8,128)S(1)} %get-tuple-element.23), channel_id=1, source_target_pairs={{0,4},{1,5},{2,6},{3,7},{4,8},{5,9},{6,10},{7,11},{8,12},{9,13},{1... | collective-permute-start | bytes 2211848 | tf_op jit(solution)/shard_map/ppermute | solution.py:41
  66.3 7.4 %collective-permute-done.13.refs_4_ = f32[4,5,24,384]{3,2,1,0:T(8,128)} collective-permute-done((f32[4,5,24,384]{3,2,1,0:T(8,128)S(1)}, f32[4,5,24,384]{3,2,1,0:T(8,128)}, u32[]{:S(2)}, u32[]{:S(2)}) %collective-permute-start.13) | collective-permute-done | bytes 737312 | tf_op jit(solution)/shard_map/ppermute | solution.py:41
  73.8 3.1 %collective-permute-start.15 = (f32[4,5,24,384]{3,2,1,0:T(8,128)}, f32[4,5,24,384]{3,2,1,0:T(8,128)}, u32[]{:S(2)}, u32[]{:S(2)}) collective-permute-start(f32[4,5,24,384]{3,2,1,0:T(8,128)} %collective-permute-done.13.refs_4_), channel_id=1, source_target_pairs={{0,28},{1,29},{2,30},{3,31},{4,0},{5,1},{6,2},{7,3},{8,4},{9,5},{1... | collective-permute-start | bytes 2211848 | tf_op jit(solution)/shard_map/ppermute | solution.py:41
  77.0 2.7 %collective-permute-start.14 = (f32[4,5,24,384]{3,2,1,0:T(8,128)S(1)}, f32[4,5,24,384]{3,2,1,0:T(8,128)}, u32[]{:S(2)}, u32[]{:S(2)}) collective-permute-start(f32[4,5,24,384]{3,2,1,0:T(8,128)S(1)} %broadcast_select_fusion), channel_id=1, source_target_pairs={{0,4},{1,5},{2,6},{3,7},{4,8},{5,9},{6,10},{7,11},{8,12},{9,13},{1... | collective-permute-start | bytes 2211848 | tf_op jit(solution)/shard_map/ppermute | solution.py:41
  79.8 1.9 %collective-permute-start.18 = (f32[4,5,24,384]{3,2,1,0:T(8,128)}, f32[4,5,24,384]{3,2,1,0:T(8,128)}, u32[]{:S(2)}, u32[]{:S(2)}) collective-permute-start(f32[4,5,24,384]{3,2,1,0:T(8,128)} %copy-done.3), channel_id=1, source_target_pairs={{0,32},{1,33},{2,34},{3,35},{4,36},{5,37},{6,38},{7,39},{8,40},{9,... | collective-permute-start | bytes 2211848 | tf_op jit(solution)/shard_map/ppermute | solution.py:41
  81.7 2.4 %collective-permute-start.20 = (f32[4,5,24,384]{3,2,1,0:T(8,128)S(1)}, f32[4,5,24,384]{3,2,1,0:T(8,128)}, u32[]{:S(2)}, u32[]{:S(2)}) collective-permute-start(f32[4,5,24,384]{3,2,1,0:T(8,128)S(1)} %collective-permute-done.11.refs_2_), channel_id=1, source_target_pairs={{0,32},{1,33},{2,34},{3,35},{4,36},{5,37},{6,38},{7,39},{8,40},{9,... | collective-permute-start | bytes 2211848 | tf_op jit(solution)/shard_map/ppermute | solution.py:41
  84.1 1.9 %collective-permute-start.19 = (f32[4,5,24,384]{3,2,1,0:T(8,128)S(1)}, f32[4,5,24,384]{3,2,1,0:T(8,128)}, u32[]{:S(2)}, u32[]{:S(2)}) collective-permute-start(f32[4,5,24,384]{3,2,1,0:T(8,128)S(1)} %collective-permute-done.10.refs_1_), channel_id=1, source_target_pairs={{0,32},{1,33},{2,34},{3,35},{4,36},{5,37},{6,38},{7,39},{8,40},{9,... | collective-permute-start | bytes 2211848 | tf_op jit(solution)/shard_map/ppermute | solution.py:41
  86.0 1.4 %collective-permute-done.15.refs_6_ = f32[4,5,24,384]{3,2,1,0:T(8,128)} collective-permute-done((f32[4,5,24,384]{3,2,1,0:T(8,128)}, f32[4,5,24,384]{3,2,1,0:T(8,128)}, u32[]{:S(2)}, u32[]{:S(2)}) %collective-permute-start.15) | collective-permute-done | bytes 737312 | tf_op jit(solution)/shard_map/ppermute | solution.py:41
  87.4 1.3 collective-permute-start.27
  88.7 3.0 %collective-permute-done.14.refs_5_ = f32[4,5,24,384]{3,2,1,0:T(8,128)} collective-permute-done((f32[4,5,24,384]{3,2,1,0:T(8,128)S(1)}, f32[4,5,24,384]{3,2,1,0:T(8,128)}, u32[]{:S(2)}, u32[]{:S(2)}) %collective-permute-start.14) | collective-permute-done | bytes 737312 | tf_op jit(solution)/shard_map/ppermute | solution.py:41
  91.7 1.9 %collective-permute-start.22 = (f32[4,5,24,384]{3,2,1,0:T(8,128)}, f32[4,5,24,384]{3,2,1,0:T(8,128)}, u32[]{:S(2)}, u32[]{:S(2)}) collective-permute-start(f32[4,5,24,384]{3,2,1,0:T(8,128)} %collective-permute-done.13.refs_4_), channel_id=1, source_target_pairs={{0,32},{1,33},{2,34},{3,35},{4,36},{5,37},{6,38},{7,39},{8,40},{9,... | collective-permute-start | bytes 2211848 | tf_op jit(solution)/shard_map/ppermute | solution.py:41
  93.7 1.8 %slice.50 = f32[2,5,24,384]{3,2,1,0:T(8,128)} slice(f32[4,5,24,384]{3,2,1,0:T(8,128)} %collective-permute-done.15.refs_6_), slice={[2:4], [0:5], [0:24], [0:384]} | slice | bytes 737280 | tf_op jit(solution)/shard_map/slice | solution.py:164
  95.4 1.0 slice.49
  96.5 2.4 %collective-permute-start.21 = (f32[4,5,24,384]{3,2,1,0:T(8,128)}, f32[4,5,24,384]{3,2,1,0:T(8,128)}, u32[]{:S(2)}, u32[]{:S(2)}) collective-permute-start(f32[4,5,24,384]{3,2,1,0:T(8,128)} %copy-done.1), channel_id=1, source_target_pairs={{0,32},{1,33},{2,34},{3,35},{4,36},{5,37},{6,38},{7,39},{8,40},{9,... | collective-permute-start | bytes 2211848 | tf_op jit(solution)/shard_map/ppermute | solution.py:41
  98.9 3.7 %collective-permute-start.17 = (f32[2,5,24,384]{3,2,1,0:T(8,128)}, f32[2,5,24,384]{3,2,1,0:T(8,128)}, u32[]{:S(2)}, u32[]{:S(2)}) collective-permute-start(f32[2,5,24,384]{3,2,1,0:T(8,128)} %slice.50), channel_id=1, source_target_pairs={{0,28},{1,29},{2,30},{3,31},{4,0},{5,1},{6,2},{7,3},{8,4},{9,5},{1... | collective-permute-start | bytes 1105928 | tf_op jit(solution)/shard_map/ppermute | solution.py:41
  102.7 2.1 %collective-permute-start.16 = (f32[2,5,24,384]{3,2,1,0:T(8,128)S(1)}, f32[2,5,24,384]{3,2,1,0:T(8,128)}, u32[]{:S(2)}, u32[]{:S(2)}) collective-permute-start(f32[2,5,24,384]{3,2,1,0:T(8,128)S(1)} %slice.49), channel_id=1, source_target_pairs={{0,4},{1,5},{2,6},{3,7},{4,8},{5,9},{6,10},{7,11},{8,12},{9,13},{1... | collective-permute-start | bytes 1105928 | tf_op jit(solution)/shard_map/ppermute | solution.py:41
  104.8 1.9 %collective-permute-start.24 = (f32[4,5,24,384]{3,2,1,0:T(8,128)}, f32[4,5,24,384]{3,2,1,0:T(8,128)}, u32[]{:S(2)}, u32[]{:S(2)}) collective-permute-start(f32[4,5,24,384]{3,2,1,0:T(8,128)} %collective-permute-done.15.refs_6_), channel_id=1, source_target_pairs={{0,32},{1,33},{2,34},{3,35},{4,36},{5,37},{6,38},{7,39},{8,40},{9,... | collective-permute-start | bytes 2211848 | tf_op jit(solution)/shard_map/ppermute | solution.py:41
  106.7 2.4 %collective-permute-start.23 = (f32[4,5,24,384]{3,2,1,0:T(8,128)}, f32[4,5,24,384]{3,2,1,0:T(8,128)}, u32[]{:S(2)}, u32[]{:S(2)}) collective-permute-start(f32[4,5,24,384]{3,2,1,0:T(8,128)} %collective-permute-done.14.refs_5_), channel_id=1, source_target_pairs={{0,32},{1,33},{2,34},{3,35},{4,36},{5,37},{6,38},{7,39},{8,40},{9,... | collective-permute-start | bytes 2211848 | tf_op jit(solution)/shard_map/ppermute | solution.py:41
  109.3 0.1 reshape.22
  109.4 0.1 reshape.23
  109.5 2.7 %collective-permute-start.26 = (f32[2,5,24,384]{3,2,1,0:T(8,128)}, f32[2,5,24,384]{3,2,1,0:T(8,128)}, u32[]{:S(2)}, u32[]{:S(2)}) collective-permute-start(f32[2,5,24,384]{3,2,1,0:T(8,128)} %collective-permute-done.17.refs_8_), channel_id=1, source_target_pairs={{0,32},{1,33},{2,34},{3,35},{4,36},{5,37},{6,38},{7,39},{8,40},{9,... | collective-permute-start | bytes 1105928 | tf_op jit(solution)/shard_map/ppermute | solution.py:41
  112.2 1.2 collective-permute-done.16.refs_7_
  113.4 2.0 %collective-permute-start.25 = (f32[2,5,24,384]{3,2,1,0:T(8,128)}, f32[2,5,24,384]{3,2,1,0:T(8,128)}, u32[]{:S(2)}, u32[]{:S(2)}) collective-permute-start(f32[2,5,24,384]{3,2,1,0:T(8,128)} %collective-permute-done.16.refs_7_), channel_id=1, source_target_pairs={{0,32},{1,33},{2,34},{3,35},{4,36},{5,37},{6,38},{7,39},{8,40},{9,... | collective-permute-start | bytes 1105928 | tf_op jit(solution)/shard_map/ppermute | solution.py:41
  115.5 0.1 copy.10
  115.6 0.1 reshape.26.mask_ref
  115.8 2.2 %localize.1.local_ref = bf16[4,512,384]{2,1,0:T(8,128)(2,1)S(1)} custom-call(s32[48]{0:T(128)S(1)} %reshape.26.mask_ref, bf16[4,512,384]{2,1,0:T(8,128)(2,1)S(1)} %copy-done, bf16[384,384]{1,0:T(8,128)(2,1)S(1)} %fusion.table_ref), custom_call_target="tpu_custom_call" | custom-call | flops 603979776 | bytes 4194304 | tf_op jit(solution)/shard_map/localize/pallas_call | solution.py:197
  118.1 17.9 %ticks.1 = f32[512,768]{1,0:T(8,128)} custom-call(s32[1]{0:T(128)} %bitcast.core_ref.where_ref, f32[512,768]{1,0:T(8,128)S(1)} %copy-done.5, bf16[4,512,384]{2,1,0:T(8,128)(2,1)S(1)} %localize.1.local_ref, f32[4,5,24,384]{3,2,1,0:T(8,128)S(1)} %copy-done.4, f32[4,5,24,384]{3,2,1,0:T(8,128)S(1)} %collective-permute-done.10.refs_1_, ...), custom_call_target="tpu_custom_call" | custom-call | flops 7247757312 | bytes 16777216 | tf_op jit(solution)/shard_map/ticks/pallas_call | solution.py:286
  (48 shorter events, 0.6 us)
Async XLA Ops:
  1.1 3.1 %collective-permute-start = (f32[24,384]{1,0:T(8,128)S(1)}, f32[24,384]{1,0:T(8,128)S(1)}, u32[]{:S(2)}, u32[]{:S(2)}) collective-permute-start(f32[24,384]{1,0:T(8,128)S(1)} %get-tuple-element.12), channel_id=1, source_target_pairs={{0,32},{1,33},{2,34},{3,35},{4,36},{5,37},{6,38},{7,39},{8,40},{9,... | collective-permute-start | bytes 110600 | tf_op jit(solution)/shard_map/ppermute | solution.py:41
  4.2 7.4 %collective-permute-start.1 = (f32[2,24,384]{2,1,0:T(8,128)S(1)}, f32[2,24,384]{2,1,0:T(8,128)S(1)}, u32[]{:S(2)}, u32[]{:S(2)}) collective-permute-start(f32[2,24,384]{2,1,0:T(8,128)S(1)} %pad_maximum_fusion.2), channel_id=1, source_target_pairs={{0,64},{1,65},{2,66},{3,67},{4,68},{5,69},{6,70},{7,71},{8,72},{9,... | collective-permute-start | bytes 221192 | tf_op jit(solution)/shard_map/ppermute | solution.py:41
  9.0 6.8 %collective-permute-start.2 = (f32[24,384]{1,0:T(8,128)S(1)}, f32[24,384]{1,0:T(8,128)S(1)}, u32[]{:S(2)}, u32[]{:S(2)}) collective-permute-start(f32[24,384]{1,0:T(8,128)S(1)} %get-tuple-element.20), channel_id=1, source_target_pairs={{0,128},{1,129},{2,130},{3,131},{4,132},{5,133},{6,134},{7,135},{8... | collective-permute-start | bytes 110600 | tf_op jit(solution)/shard_map/ppermute | solution.py:41
  15.7 11.4 %collective-permute-start.9 = (f32[5,24,384]{2,1,0:T(8,128)S(1)}, f32[5,24,384]{2,1,0:T(8,128)S(1)}, u32[]{:S(2)}, u32[]{:S(2)}) collective-permute-start(f32[5,24,384]{2,1,0:T(8,128)S(1)} %bitcast_dynamic-update-slice_fusion), channel_id=1, source_target_pairs={{0,1},{1,2},{2,3},{3,0},{4,5},{5,6},{6,7},{7,4},{8,9},{9,10},{10,1... | collective-permute-start | bytes 552968 | tf_op jit(solution)/shard_map/ppermute | solution.py:41
  19.1 8.9 %collective-permute-start.5 = (f32[5,24,384]{2,1,0:T(8,128)S(1)}, f32[5,24,384]{2,1,0:T(8,128)S(1)}, u32[]{:S(2)}, u32[]{:S(2)}) collective-permute-start(f32[5,24,384]{2,1,0:T(8,128)S(1)} %bitcast_dynamic-update-slice_fusion), channel_id=1, source_target_pairs={{0,2},{1,3},{2,0},{3,1},{4,6},{5,7},{6,4},{7,5},{8,10},{9,11},{10,... | collective-permute-start | bytes 552968 | tf_op jit(solution)/shard_map/ppermute | solution.py:41
  23.8 7.4 %collective-permute-start.3 = (f32[5,24,384]{2,1,0:T(8,128)S(1)}, f32[5,24,384]{2,1,0:T(8,128)S(1)}, u32[]{:S(2)}, u32[]{:S(2)}) collective-permute-start(f32[5,24,384]{2,1,0:T(8,128)S(1)} %bitcast_dynamic-update-slice_fusion), channel_id=1, source_target_pairs={{0,3},{1,0},{2,1},{3,2},{4,7},{5,4},{6,5},{7,6},{8,11},{9,8},{10,9... | collective-permute-start | bytes 552968 | tf_op jit(solution)/shard_map/ppermute | solution.py:41
  31.3 30.9 %copy-start.3 = (f32[4,5,24,384]{3,2,1,0:T(8,128)}, f32[4,5,24,384]{3,2,1,0:T(8,128)S(1)}, u32[]{:S(2)}) copy-start(f32[4,5,24,384]{3,2,1,0:T(8,128)S(1)} %pad_maximum_fusion.1.refs_0_) | copy-start | bytes 2211844
  31.3 22.2 %collective-permute-start.11 = (f32[4,5,24,384]{3,2,1,0:T(8,128)S(1)}, f32[4,5,24,384]{3,2,1,0:T(8,128)S(1)}, u32[]{:S(2)}, u32[]{:S(2)}) collective-permute-start(f32[4,5,24,384]{3,2,1,0:T(8,128)S(1)} %pad_maximum_fusion.1.refs_0_), channel_id=1, source_target_pairs={{0,28},{1,29},{2,30},{3,31},{4,0},{5,1},{6,2},{7,3},{8,4},{9,5},{1... | collective-permute-start | bytes 2211848 | tf_op jit(solution)/shard_map/ppermute | solution.py:41
  42.6 16.5 %collective-permute-start.10 = (f32[4,5,24,384]{3,2,1,0:T(8,128)S(1)}, f32[4,5,24,384]{3,2,1,0:T(8,128)S(1)}, u32[]{:S(2)}, u32[]{:S(2)}) collective-permute-start(f32[4,5,24,384]{3,2,1,0:T(8,128)S(1)} %pad_maximum_fusion.1.refs_0_), channel_id=1, source_target_pairs={{0,4},{1,5},{2,6},{3,7},{4,8},{5,9},{6,10},{7,11},{8,12},{9,13},{1... | collective-permute-start | bytes 2211848 | tf_op jit(solution)/shard_map/ppermute | solution.py:41
  44.5 1.4 %collective-permute-start.6 = (f32[5,24,384]{2,1,0:T(8,128)S(1)}, f32[5,24,384]{2,1,0:T(8,128)S(1)}, u32[]{:S(2)}, u32[]{:S(2)}) collective-permute-start(f32[5,24,384]{2,1,0:T(8,128)S(1)} %collective-permute-done.5), channel_id=1, source_target_pairs={{32,36},{33,37},{34,38},{35,39},{36,40},{37,41},{38,42},{39,43},{4... | collective-permute-start | bytes 552968 | tf_op jit(solution)/shard_map/ppermute | solution.py:41
  45.2 1.4 %collective-permute-start.4 = (f32[5,24,384]{2,1,0:T(8,128)S(1)}, f32[5,24,384]{2,1,0:T(8,128)S(1)}, u32[]{:S(2)}, u32[]{:S(2)}) collective-permute-start(f32[5,24,384]{2,1,0:T(8,128)S(1)} %collective-permute-done.3), channel_id=1, source_target_pairs={{32,60},{33,61},{34,62},{35,63},{36,32},{37,33},{38,34},{39,35},{4... | collective-permute-start | bytes 552968 | tf_op jit(solution)/shard_map/ppermute | solution.py:41
  45.9 1.4 %collective-permute-start.8 = (f32[5,24,384]{2,1,0:T(8,128)S(1)}, f32[5,24,384]{2,1,0:T(8,128)S(1)}, u32[]{:S(2)}, u32[]{:S(2)}) collective-permute-start(f32[5,24,384]{2,1,0:T(8,128)S(1)} %collective-permute-done.6), channel_id=1, source_target_pairs={{32,36},{33,37},{34,38},{35,39},{36,40},{37,41},{38,42},{39,43},{4... | collective-permute-start | bytes 552968 | tf_op jit(solution)/shard_map/ppermute | solution.py:41
  46.6 0.7 collective-permute-start.7
  60.2 33.5 %copy-start.7 = (s32[2,32,2]{1,2,0:T(2,128)S(1)}, s32[2,32,2]{1,2,0:T(2,128)}, u32[]{:S(2)}) copy-start(s32[2,32,2]{1,2,0:T(2,128)} %constant.77.clone) | copy-start | bytes 1540
  60.2 13.6 %collective-permute-start.13 = (f32[4,5,24,384]{3,2,1,0:T(8,128)S(1)}, f32[4,5,24,384]{3,2,1,0:T(8,128)}, u32[]{:S(2)}, u32[]{:S(2)}) collective-permute-start(f32[4,5,24,384]{3,2,1,0:T(8,128)S(1)} %get-tuple-element.21), channel_id=1, source_target_pairs={{0,28},{1,29},{2,30},{3,31},{4,0},{5,1},{6,2},{7,3},{8,4},{9,5},{1... | collective-permute-start | bytes 2211848 | tf_op jit(solution)/shard_map/ppermute | solution.py:41
  62.2 53.3 %copy-start.6 = (s32[4,4,3]{1,0,2:T(4,128)S(1)}, s32[4,4,3]{1,0,2:T(4,128)}, u32[]{:S(2)}) copy-start(s32[4,4,3]{1,0,2:T(4,128)} %param.10) | copy-start | bytes 580
  62.2 53.5 %copy-start = (bf16[4,512,384]{2,1,0:T(8,128)(2,1)S(1)}, bf16[4,512,384]{2,1,0:T(8,128)(2,1)}, u32[]{:S(2)}) copy-start(bf16[4,512,384]{2,1,0:T(8,128)(2,1)} %taper_ref) | copy-start | bytes 4718596
  62.3 14.7 %collective-permute-start.12 = (f32[4,5,24,384]{3,2,1,0:T(8,128)S(1)}, f32[4,5,24,384]{3,2,1,0:T(8,128)S(1)}, u32[]{:S(2)}, u32[]{:S(2)}) collective-permute-start(f32[4,5,24,384]{3,2,1,0:T(8,128)S(1)} %get-tuple-element.23), channel_id=1, source_target_pairs={{0,4},{1,5},{2,6},{3,7},{4,8},{5,9},{6,10},{7,11},{8,12},{9,13},{1... | collective-permute-start | bytes 2211848 | tf_op jit(solution)/shard_map/ppermute | solution.py:41
  73.8 13.7 %collective-permute-start.15 = (f32[4,5,24,384]{3,2,1,0:T(8,128)}, f32[4,5,24,384]{3,2,1,0:T(8,128)}, u32[]{:S(2)}, u32[]{:S(2)}) collective-permute-start(f32[4,5,24,384]{3,2,1,0:T(8,128)} %collective-permute-done.13.refs_4_), channel_id=1, source_target_pairs={{0,28},{1,29},{2,30},{3,31},{4,0},{5,1},{6,2},{7,3},{8,4},{9,5},{1... | collective-permute-start | bytes 2211848 | tf_op jit(solution)/shard_map/ppermute | solution.py:41
  77.0 4.7 %copy-start.1 = (f32[4,5,24,384]{3,2,1,0:T(8,128)}, f32[4,5,24,384]{3,2,1,0:T(8,128)S(1)}, u32[]{:S(2)}) copy-start(f32[4,5,24,384]{3,2,1,0:T(8,128)S(1)} %collective-permute-done.12.refs_3_) | copy-start | bytes 2211844
  77.0 14.7 %collective-permute-start.14 = (f32[4,5,24,384]{3,2,1,0:T(8,128)S(1)}, f32[4,5,24,384]{3,2,1,0:T(8,128)}, u32[]{:S(2)}, u32[]{:S(2)}) collective-permute-start(f32[4,5,24,384]{3,2,1,0:T(8,128)S(1)} %broadcast_select_fusion), channel_id=1, source_target_pairs={{0,4},{1,5},{2,6},{3,7},{4,8},{5,9},{6,10},{7,11},{8,12},{9,13},{1... | collective-permute-start | bytes 2211848 | tf_op jit(solution)/shard_map/ppermute | solution.py:41
  79.8 16.7 %collective-permute-start.18 = (f32[4,5,24,384]{3,2,1,0:T(8,128)}, f32[4,5,24,384]{3,2,1,0:T(8,128)}, u32[]{:S(2)}, u32[]{:S(2)}) collective-permute-start(f32[4,5,24,384]{3,2,1,0:T(8,128)} %copy-done.3), channel_id=1, source_target_pairs={{0,32},{1,33},{2,34},{3,35},{4,36},{5,37},{6,38},{7,39},{8,40},{9,... | collective-permute-start | bytes 2211848 | tf_op jit(solution)/shard_map/ppermute | solution.py:41
  81.7 17.2 %collective-permute-start.20 = (f32[4,5,24,384]{3,2,1,0:T(8,128)S(1)}, f32[4,5,24,384]{3,2,1,0:T(8,128)}, u32[]{:S(2)}, u32[]{:S(2)}) collective-permute-start(f32[4,5,24,384]{3,2,1,0:T(8,128)S(1)} %collective-permute-done.11.refs_2_), channel_id=1, source_target_pairs={{0,32},{1,33},{2,34},{3,35},{4,36},{5,37},{6,38},{7,39},{8,40},{9,... | collective-permute-start | bytes 2211848 | tf_op jit(solution)/shard_map/ppermute | solution.py:41
  84.1 18.5 %collective-permute-start.19 = (f32[4,5,24,384]{3,2,1,0:T(8,128)S(1)}, f32[4,5,24,384]{3,2,1,0:T(8,128)}, u32[]{:S(2)}, u32[]{:S(2)}) collective-permute-start(f32[4,5,24,384]{3,2,1,0:T(8,128)S(1)} %collective-permute-done.10.refs_1_), channel_id=1, source_target_pairs={{0,32},{1,33},{2,34},{3,35},{4,36},{5,37},{6,38},{7,39},{8,40},{9,... | collective-permute-start | bytes 2211848 | tf_op jit(solution)/shard_map/ppermute | solution.py:41
  87.4 17.3 %collective-permute-start.27 = (f32[4,5,24,384]{3,2,1,0:T(8,128)}, f32[4,5,24,384]{3,2,1,0:T(8,128)}, u32[]{:S(2)}, u32[]{:S(2)}) collective-permute-start(f32[4,5,24,384]{3,2,1,0:T(8,128)} %get-tuple-element.22.refs_9_), channel_id=1, source_target_pairs={{32,0},{33,1},{34,2},{35,3},{36,4},{37,5},{38,6},{39,7},{40,8},{41... | collective-permute-start | bytes 2211848 | tf_op jit(solution)/shard_map/ppermute | solution.py:41
  91.7 15.0 %collective-permute-start.22 = (f32[4,5,24,384]{3,2,1,0:T(8,128)}, f32[4,5,24,384]{3,2,1,0:T(8,128)}, u32[]{:S(2)}, u32[]{:S(2)}) collective-permute-start(f32[4,5,24,384]{3,2,1,0:T(8,128)} %collective-permute-done.13.refs_4_), channel_id=1, source_target_pairs={{0,32},{1,33},{2,34},{3,35},{4,36},{5,37},{6,38},{7,39},{8,40},{9,... | collective-permute-start | bytes 2211848 | tf_op jit(solution)/shard_map/ppermute | solution.py:41
  96.5 21.5 %collective-permute-start.21 = (f32[4,5,24,384]{3,2,1,0:T(8,128)}, f32[4,5,24,384]{3,2,1,0:T(8,128)}, u32[]{:S(2)}, u32[]{:S(2)}) collective-permute-start(f32[4,5,24,384]{3,2,1,0:T(8,128)} %copy-done.1), channel_id=1, source_target_pairs={{0,32},{1,33},{2,34},{3,35},{4,36},{5,37},{6,38},{7,39},{8,40},{9,... | collective-permute-start | bytes 2211848 | tf_op jit(solution)/shard_map/ppermute | solution.py:41
  98.9 10.6 %collective-permute-start.17 = (f32[2,5,24,384]{3,2,1,0:T(8,128)}, f32[2,5,24,384]{3,2,1,0:T(8,128)}, u32[]{:S(2)}, u32[]{:S(2)}) collective-permute-start(f32[2,5,24,384]{3,2,1,0:T(8,128)} %slice.50), channel_id=1, source_target_pairs={{0,28},{1,29},{2,30},{3,31},{4,0},{5,1},{6,2},{7,3},{8,4},{9,5},{1... | collective-permute-start | bytes 1105928 | tf_op jit(solution)/shard_map/ppermute | solution.py:41
  102.7 10.7 %collective-permute-start.16 = (f32[2,5,24,384]{3,2,1,0:T(8,128)S(1)}, f32[2,5,24,384]{3,2,1,0:T(8,128)}, u32[]{:S(2)}, u32[]{:S(2)}) collective-permute-start(f32[2,5,24,384]{3,2,1,0:T(8,128)S(1)} %slice.49), channel_id=1, source_target_pairs={{0,4},{1,5},{2,6},{3,7},{4,8},{5,9},{6,10},{7,11},{8,12},{9,13},{1... | collective-permute-start | bytes 1105928 | tf_op jit(solution)/shard_map/ppermute | solution.py:41
  104.8 13.2 %collective-permute-start.24 = (f32[4,5,24,384]{3,2,1,0:T(8,128)}, f32[4,5,24,384]{3,2,1,0:T(8,128)}, u32[]{:S(2)}, u32[]{:S(2)}) collective-permute-start(f32[4,5,24,384]{3,2,1,0:T(8,128)} %collective-permute-done.15.refs_6_), channel_id=1, source_target_pairs={{0,32},{1,33},{2,34},{3,35},{4,36},{5,37},{6,38},{7,39},{8,40},{9,... | collective-permute-start | bytes 2211848 | tf_op jit(solution)/shard_map/ppermute | solution.py:41
  106.7 11.3 %collective-permute-start.23 = (f32[4,5,24,384]{3,2,1,0:T(8,128)}, f32[4,5,24,384]{3,2,1,0:T(8,128)}, u32[]{:S(2)}, u32[]{:S(2)}) collective-permute-start(f32[4,5,24,384]{3,2,1,0:T(8,128)} %collective-permute-done.14.refs_5_), channel_id=1, source_target_pairs={{0,32},{1,33},{2,34},{3,35},{4,36},{5,37},{6,38},{7,39},{8,40},{9,... | collective-permute-start | bytes 2211848 | tf_op jit(solution)/shard_map/ppermute | solution.py:41
  109.5 8.5 %collective-permute-start.26 = (f32[2,5,24,384]{3,2,1,0:T(8,128)}, f32[2,5,24,384]{3,2,1,0:T(8,128)}, u32[]{:S(2)}, u32[]{:S(2)}) collective-permute-start(f32[2,5,24,384]{3,2,1,0:T(8,128)} %collective-permute-done.17.refs_8_), channel_id=1, source_target_pairs={{0,32},{1,33},{2,34},{3,35},{4,36},{5,37},{6,38},{7,39},{8,40},{9,... | collective-permute-start | bytes 1105928 | tf_op jit(solution)/shard_map/ppermute | solution.py:41
  113.4 4.7 %collective-permute-start.25 = (f32[2,5,24,384]{3,2,1,0:T(8,128)}, f32[2,5,24,384]{3,2,1,0:T(8,128)}, u32[]{:S(2)}, u32[]{:S(2)}) collective-permute-start(f32[2,5,24,384]{3,2,1,0:T(8,128)} %collective-permute-done.16.refs_7_), channel_id=1, source_target_pairs={{0,32},{1,33},{2,34},{3,35},{4,36},{5,37},{6,38},{7,39},{8,40},{9,... | collective-permute-start | bytes 1105928 | tf_op jit(solution)/shard_map/ppermute | solution.py:41
  115.7 2.3 %copy-start.2 = (f32[4,5,24,384]{3,2,1,0:T(8,128)S(1)}, f32[4,5,24,384]{3,2,1,0:T(8,128)}, u32[]{:S(2)}) copy-start(f32[4,5,24,384]{3,2,1,0:T(8,128)} %copy-done.1) | copy-start | bytes 2211844
  115.7 2.3 %copy-start.4 = (f32[4,5,24,384]{3,2,1,0:T(8,128)S(1)}, f32[4,5,24,384]{3,2,1,0:T(8,128)}, u32[]{:S(2)}) copy-start(f32[4,5,24,384]{3,2,1,0:T(8,128)} %copy-done.3) | copy-start | bytes 2211844
  115.7 2.3 %copy-start.5 = (f32[512,768]{1,0:T(8,128)S(1)}, f32[512,768]{1,0:T(8,128)}, u32[]{:S(2)}) copy-start(f32[512,768]{1,0:T(8,128)} %state_ref.1) | copy-start | bytes 4718596

commit v4 on v3

--- a/solution.py
+++ b/solution.py
@@ -149,15 +149,16 @@
     n6 = send(n4, only_down)
     n7 = send(n5, only_up)
     high = jnp.stack([n4, n5, n6, n7])
-    up2 = send(jnp.where(first, up1, high), up)
+    held = jnp.where(first, up1, high)
+    up2 = send(held, up)
     down2 = send(jnp.where(first, down1, high), down)
     par_low = send(low, flip)
     par_up1 = send(up1, flip)
     par_down1 = send(down1, flip)
-    local = make_local(high)
+    local = make_local(held)
     up3 = send(jnp.where(first, up2, up1), up)
     down3 = send(down2, down)
-    par_high = send(high, to_first)
+    par_high = send(held, to_first)
     par_up2 = send(up2, flip)
     par_down2 = send(down2, flip)
     far_up = send(up3[:2], both((1, 0), None))
@@ -166,7 +167,7 @@
     par_down3 = send(down3, flip)
     par_far_up = send(far_up, to_second)
     par_far_down = send(far_down, to_second)
-    own = [low, up1, down1, up2, down2, up3, down3, far_up, far_down, high]
+    own = [low, up1, down1, up2, down2, up3, down3, far_up, far_down, held]
     par = [par_low, par_up1, par_down1, par_up2, par_down2, par_up3, par_down3, par_far_up, par_far_down, par_high]
     return own, par, local
 
@@ -298,7 +299,7 @@
             scratch_shapes=[pltpu.VMEM((OBS, 3 * MEMBERS), BF16), pltpu.VMEM((3 * OBS, MEMBERS), BF16)],
         ),
         cost_estimate=pl.CostEstimate(flops=48 * ROWS * SLOTS * MEMBERS, bytes_accessed=16 << 20, transcendentals=0),
-        compiler_params=pltpu.CompilerParams(vmem_limit_bytes=28 << 20),
+        compiler_params=pltpu.CompilerParams(vmem_limit_bytes=22 << 20),
         name="ticks",
     )(core.reshape(1), state, local, *own, *par)
 

time: 137 us -> 140 us (1.022)
  starting transfers between devices: 75.3 us -> 76.8 us
    ppermute x28, starting transfers between devices: 75.3 us -> 76.8 us  [send(): return lax.ppermute(block, ('region', 'var'), route(move))]
where the time goes in v4:
time: 140 us; the launch traced here: 139 us
  starting transfers between devices  76.8 us (55%)
  waiting for transfers between devices  35.6 us (25%)
  Pallas kernels  21.2 us (15%)
  local copies, waits for them, and re-layouts  3.29 us (2%)
    ppermute x28, starting transfers between devices, send(): return lax.ppermute(block, ('region', 'var'), route(move))  76.8 us
    ppermute x28, waiting for transfers between devices, send(): return lax.ppermute(block, ('region', 'var'), route(move))  35.6 us
    pallas_call x1, Pallas kernels, run_ticks(): pl.pallas_call(ticks_kernel, out_shape=jax.ShapeDtypeStruct((ROWS, MEMBER...  17.9 us
  transfers between devices with their start and end apart: 28, of which 11 were waited for; matrix products, arithmetic and copies ran while one was open for 3% of the time, Pallas kernels for 2%

profile of v4, /device:TPU:24, one launch (start us, length us, event | category | flops | bytes accessed | tf_op | source)
XLA Modules:
  0.0 138.9 jit_solution(9368750343488648408)
XLA Ops:
  0.0 1.1 pack.1
  1.1 1.9 %collective-permute-start = (f32[24,384]{1,0:T(8,128)S(1)}, f32[24,384]{1,0:T(8,128)S(1)}, u32[]{:S(2)}, u32[]{:S(2)}) collective-permute-start(f32[24,384]{1,0:T(8,128)S(1)} %get-tuple-element.12), channel_id=1, source_target_pairs={{0,32},{1,33},{2,34},{3,35},{4,36},{5,37},{6,38},{7,39},{8,40},{9,... | collective-permute-start | bytes 110600 | tf_op jit(solution)/shard_map/ppermute | solution.py:41
  3.0 1.2 collective-permute-done
  4.2 4.7 %collective-permute-start.1 = (f32[2,24,384]{2,1,0:T(8,128)S(1)}, f32[2,24,384]{2,1,0:T(8,128)S(1)}, u32[]{:S(2)}, u32[]{:S(2)}) collective-permute-start(f32[2,24,384]{2,1,0:T(8,128)S(1)} %pad_maximum_fusion.2), channel_id=1, source_target_pairs={{0,64},{1,65},{2,66},{3,67},{4,68},{5,69},{6,70},{7,71},{8,72},{9,... | collective-permute-start | bytes 221192 | tf_op jit(solution)/shard_map/ppermute | solution.py:41
  9.0 2.7 %collective-permute-start.2 = (f32[24,384]{1,0:T(8,128)S(1)}, f32[24,384]{1,0:T(8,128)S(1)}, u32[]{:S(2)}, u32[]{:S(2)}) collective-permute-start(f32[24,384]{1,0:T(8,128)S(1)} %get-tuple-element.20), channel_id=1, source_target_pairs={{0,128},{1,129},{2,130},{3,131},{4,132},{5,133},{6,134},{7,135},{8... | collective-permute-start | bytes 110600 | tf_op jit(solution)/shard_map/ppermute | solution.py:41
  11.7 4.0 %collective-permute-done.2 = f32[24,384]{1,0:T(8,128)S(1)} collective-permute-done((f32[24,384]{1,0:T(8,128)S(1)}, f32[24,384]{1,0:T(8,128)S(1)}, u32[]{:S(2)}, u32[]{:S(2)}) %collective-permute-start.2) | collective-permute-done | bytes 36896 | tf_op jit(solution)/shard_map/ppermute | solution.py:41
  15.7 4.9 %collective-permute-start.5 = (f32[5,24,384]{2,1,0:T(8,128)S(1)}, f32[5,24,384]{2,1,0:T(8,128)S(1)}, u32[]{:S(2)}, u32[]{:S(2)}) collective-permute-start(f32[5,24,384]{2,1,0:T(8,128)S(1)} %bitcast_dynamic-update-slice_fusion), channel_id=1, source_target_pairs={{0,2},{1,3},{2,0},{3,1},{4,6},{5,7},{6,4},{7,5},{8,10},{9,11},{10,... | collective-permute-start | bytes 552968 | tf_op jit(solution)/shard_map/ppermute | solution.py:41
  20.7 3.0 %collective-permute-start.4 = (f32[5,24,384]{2,1,0:T(8,128)S(1)}, f32[5,24,384]{2,1,0:T(8,128)S(1)}, u32[]{:S(2)}, u32[]{:S(2)}) collective-permute-start(f32[5,24,384]{2,1,0:T(8,128)S(1)} %bitcast_dynamic-update-slice_fusion), channel_id=1, source_target_pairs={{0,3},{1,0},{2,1},{3,2},{4,7},{5,4},{6,5},{7,6},{8,11},{9,8},{10,9... | collective-permute-start | bytes 552968 | tf_op jit(solution)/shard_map/ppermute | solution.py:41
  23.7 2.8 %collective-permute-start.3 = (f32[5,24,384]{2,1,0:T(8,128)S(1)}, f32[5,24,384]{2,1,0:T(8,128)S(1)}, u32[]{:S(2)}, u32[]{:S(2)}) collective-permute-start(f32[5,24,384]{2,1,0:T(8,128)S(1)} %bitcast_dynamic-update-slice_fusion), channel_id=1, source_target_pairs={{0,1},{1,2},{2,3},{3,0},{4,5},{5,6},{6,7},{7,4},{8,9},{9,10},{10,1... | collective-permute-start | bytes 552968 | tf_op jit(solution)/shard_map/ppermute | solution.py:41
  26.5 1.6 %collective-permute-done.4 = f32[5,24,384]{2,1,0:T(8,128)S(1)} collective-permute-done((f32[5,24,384]{2,1,0:T(8,128)S(1)}, f32[5,24,384]{2,1,0:T(8,128)S(1)}, u32[]{:S(2)}, u32[]{:S(2)}) %collective-permute-start.4) | collective-permute-done | bytes 184352 | tf_op jit(solution)/shard_map/ppermute | solution.py:41
  28.1 4.3 %collective-permute-done.3 = f32[5,24,384]{2,1,0:T(8,128)S(1)} collective-permute-done((f32[5,24,384]{2,1,0:T(8,128)S(1)}, f32[5,24,384]{2,1,0:T(8,128)S(1)}, u32[]{:S(2)}, u32[]{:S(2)}) %collective-permute-start.3) | collective-permute-done | bytes 184352 | tf_op jit(solution)/shard_map/ppermute | solution.py:41
  32.4 10.9 %collective-permute-start.11 = (f32[4,5,24,384]{3,2,1,0:T(8,128)S(1)}, f32[4,5,24,384]{3,2,1,0:T(8,128)S(1)}, u32[]{:S(2)}, u32[]{:S(2)}) collective-permute-start(f32[4,5,24,384]{3,2,1,0:T(8,128)S(1)} %pad_maximum_fusion.refs_0_), channel_id=1, source_target_pairs={{0,28},{1,29},{2,30},{3,31},{4,0},{5,1},{6,2},{7,3},{8,4},{9,5},{1... | collective-permute-start | bytes 2211848 | tf_op jit(solution)/shard_map/ppermute | solution.py:41
  43.4 1.9 %collective-permute-start.6 = (f32[4,5,24,384]{3,2,1,0:T(8,128)S(1)}, f32[4,5,24,384]{3,2,1,0:T(8,128)S(1)}, u32[]{:S(2)}, u32[]{:S(2)}) collective-permute-start(f32[4,5,24,384]{3,2,1,0:T(8,128)S(1)} %pad_maximum_fusion.refs_0_), channel_id=1, source_target_pairs={{0,4},{1,5},{2,6},{3,7},{4,8},{5,9},{6,10},{7,11},{8,12},{9,13},{1... | collective-permute-start | bytes 2211848 | tf_op jit(solution)/shard_map/ppermute | solution.py:41
  45.3 0.7 collective-permute-start.8
  46.0 0.7 collective-permute-start.7
  46.7 0.7 collective-permute-start.10
  47.4 0.7 collective-permute-start.9
  48.1 6.2 %collective-permute-done.11.refs_2_ = f32[4,5,24,384]{3,2,1,0:T(8,128)S(1)} collective-permute-done((f32[4,5,24,384]{3,2,1,0:T(8,128)S(1)}, f32[4,5,24,384]{3,2,1,0:T(8,128)S(1)}, u32[]{:S(2)}, u32[]{:S(2)}) %collective-permute-start.11) | collective-permute-done | bytes 737312 | tf_op jit(solution)/shard_map/ppermute | solution.py:41
  54.3 5.6 %collective-permute-done.6.refs_1_ = f32[4,5,24,384]{3,2,1,0:T(8,128)S(1)} collective-permute-done((f32[4,5,24,384]{3,2,1,0:T(8,128)S(1)}, f32[4,5,24,384]{3,2,1,0:T(8,128)S(1)}, u32[]{:S(2)}, u32[]{:S(2)}) %collective-permute-start.6) | collective-permute-done | bytes 737312 | tf_op jit(solution)/shard_map/ppermute | solution.py:41
  59.9 1.0 fusion.1
  61.0 2.0 %collective-permute-start.13 = (f32[4,5,24,384]{3,2,1,0:T(8,128)S(1)}, f32[4,5,24,384]{3,2,1,0:T(8,128)}, u32[]{:S(2)}, u32[]{:S(2)}) collective-permute-start(f32[4,5,24,384]{3,2,1,0:T(8,128)S(1)} %get-tuple-element.21), channel_id=1, source_target_pairs={{0,28},{1,29},{2,30},{3,31},{4,0},{5,1},{6,2},{7,3},{8,4},{9,5},{1... | collective-permute-start | bytes 2211848 | tf_op jit(solution)/shard_map/ppermute | solution.py:41
  63.1 4.1 %collective-permute-start.12 = (f32[4,5,24,384]{3,2,1,0:T(8,128)}, f32[4,5,24,384]{3,2,1,0:T(8,128)S(1)}, u32[]{:S(2)}, u32[]{:S(2)}) collective-permute-start(f32[4,5,24,384]{3,2,1,0:T(8,128)} %get-tuple-element.22.refs_9_), channel_id=1, source_target_pairs={{0,4},{1,5},{2,6},{3,7},{4,8},{5,9},{6,10},{7,11},{8,12},{9,13},{1... | collective-permute-start | bytes 2211848 | tf_op jit(solution)/shard_map/ppermute | solution.py:41
  67.1 7.4 %collective-permute-done.13.refs_4_ = f32[4,5,24,384]{3,2,1,0:T(8,128)} collective-permute-done((f32[4,5,24,384]{3,2,1,0:T(8,128)S(1)}, f32[4,5,24,384]{3,2,1,0:T(8,128)}, u32[]{:S(2)}, u32[]{:S(2)}) %collective-permute-start.13) | collective-permute-done | bytes 737312 | tf_op jit(solution)/shard_map/ppermute | solution.py:41
  74.6 3.1 %collective-permute-start.15 = (f32[4,5,24,384]{3,2,1,0:T(8,128)}, f32[4,5,24,384]{3,2,1,0:T(8,128)}, u32[]{:S(2)}, u32[]{:S(2)}) collective-permute-start(f32[4,5,24,384]{3,2,1,0:T(8,128)} %collective-permute-done.13.refs_4_), channel_id=1, source_target_pairs={{0,28},{1,29},{2,30},{3,31},{4,0},{5,1},{6,2},{7,3},{8,4},{9,5},{1... | collective-permute-start | bytes 2211848 | tf_op jit(solution)/shard_map/ppermute | solution.py:41
  77.7 0.3 collective-permute-done.12.refs_3_
  78.1 2.7 %collective-permute-start.14 = (f32[4,5,24,384]{3,2,1,0:T(8,128)S(1)}, f32[4,5,24,384]{3,2,1,0:T(8,128)}, u32[]{:S(2)}, u32[]{:S(2)}) collective-permute-start(f32[4,5,24,384]{3,2,1,0:T(8,128)S(1)} %broadcast_select_fusion), channel_id=1, source_target_pairs={{0,4},{1,5},{2,6},{3,7},{4,8},{5,9},{6,10},{7,11},{8,12},{9,13},{1... | collective-permute-start | bytes 2211848 | tf_op jit(solution)/shard_map/ppermute | solution.py:41
  80.8 2.7 %collective-permute-start.18 = (f32[4,5,24,384]{3,2,1,0:T(8,128)}, f32[4,5,24,384]{3,2,1,0:T(8,128)}, u32[]{:S(2)}, u32[]{:S(2)}) collective-permute-start(f32[4,5,24,384]{3,2,1,0:T(8,128)} %copy-done.1), channel_id=1, source_target_pairs={{0,32},{1,33},{2,34},{3,35},{4,36},{5,37},{6,38},{7,39},{8,40},{9,... | collective-permute-start | bytes 2211848 | tf_op jit(solution)/shard_map/ppermute | solution.py:41
  83.5 1.9 %collective-permute-start.20 = (f32[4,5,24,384]{3,2,1,0:T(8,128)}, f32[4,5,24,384]{3,2,1,0:T(8,128)}, u32[]{:S(2)}, u32[]{:S(2)}) collective-permute-start(f32[4,5,24,384]{3,2,1,0:T(8,128)} %copy-done.3), channel_id=1, source_target_pairs={{0,32},{1,33},{2,34},{3,35},{4,36},{5,37},{6,38},{7,39},{8,40},{9,... | collective-permute-start | bytes 2211848 | tf_op jit(solution)/shard_map/ppermute | solution.py:41
  85.4 1.3 collective-permute-start.27
  86.7 1.5 %collective-permute-done.15.refs_6_ = f32[4,5,24,384]{3,2,1,0:T(8,128)} collective-permute-done((f32[4,5,24,384]{3,2,1,0:T(8,128)}, f32[4,5,24,384]{3,2,1,0:T(8,128)}, u32[]{:S(2)}, u32[]{:S(2)}) %collective-permute-start.15) | collective-permute-done | bytes 737312 | tf_op jit(solution)/shard_map/ppermute | solution.py:41
  88.2 2.4 %collective-permute-start.19 = (f32[4,5,24,384]{3,2,1,0:T(8,128)S(1)}, f32[4,5,24,384]{3,2,1,0:T(8,128)}, u32[]{:S(2)}, u32[]{:S(2)}) collective-permute-start(f32[4,5,24,384]{3,2,1,0:T(8,128)S(1)} %collective-permute-done.6.refs_1_), channel_id=1, source_target_pairs={{0,32},{1,33},{2,34},{3,35},{4,36},{5,37},{6,38},{7,39},{8,40},{9,... | collective-permute-start | bytes 2211848 | tf_op jit(solution)/shard_map/ppermute | solution.py:41
  90.6 2.1 %collective-permute-done.14.refs_5_ = f32[4,5,24,384]{3,2,1,0:T(8,128)} collective-permute-done((f32[4,5,24,384]{3,2,1,0:T(8,128)S(1)}, f32[4,5,24,384]{3,2,1,0:T(8,128)}, u32[]{:S(2)}, u32[]{:S(2)}) %collective-permute-start.14) | collective-permute-done | bytes 737312 | tf_op jit(solution)/shard_map/ppermute | solution.py:41
  92.7 2.3 %collective-permute-start.22 = (f32[4,5,24,384]{3,2,1,0:T(8,128)}, f32[4,5,24,384]{3,2,1,0:T(8,128)}, u32[]{:S(2)}, u32[]{:S(2)}) collective-permute-start(f32[4,5,24,384]{3,2,1,0:T(8,128)} %collective-permute-done.13.refs_4_), channel_id=1, source_target_pairs={{0,32},{1,33},{2,34},{3,35},{4,36},{5,37},{6,38},{7,39},{8,40},{9,... | collective-permute-start | bytes 2211848 | tf_op jit(solution)/shard_map/ppermute | solution.py:41
  95.1 1.8 %slice.50 = f32[2,5,24,384]{3,2,1,0:T(8,128)} slice(f32[4,5,24,384]{3,2,1,0:T(8,128)} %collective-permute-done.15.refs_6_), slice={[2:4], [0:5], [0:24], [0:384]} | slice | bytes 737280 | tf_op jit(solution)/shard_map/slice | solution.py:165
  96.9 1.0 slice.49
  97.9 2.0 %collective-permute-start.21 = (f32[4,5,24,384]{3,2,1,0:T(8,128)S(1)}, f32[4,5,24,384]{3,2,1,0:T(8,128)}, u32[]{:S(2)}, u32[]{:S(2)}) collective-permute-start(f32[4,5,24,384]{3,2,1,0:T(8,128)S(1)} %collective-permute-done.12.refs_3_), channel_id=1, source_target_pairs={{0,32},{1,33},{2,34},{3,35},{4,36},{5,37},{6,38},{7,39},{8,40},{9,... | collective-permute-start | bytes 2211848 | tf_op jit(solution)/shard_map/ppermute | solution.py:41
  99.9 5.6 %collective-permute-start.17 = (f32[2,5,24,384]{3,2,1,0:T(8,128)}, f32[2,5,24,384]{3,2,1,0:T(8,128)}, u32[]{:S(2)}, u32[]{:S(2)}) collective-permute-start(f32[2,5,24,384]{3,2,1,0:T(8,128)} %slice.50), channel_id=1, source_target_pairs={{0,28},{1,29},{2,30},{3,31},{4,0},{5,1},{6,2},{7,3},{8,4},{9,5},{1... | collective-permute-start | bytes 1105928 | tf_op jit(solution)/shard_map/ppermute | solution.py:41
  105.6 1.9 %collective-permute-start.16 = (f32[2,5,24,384]{3,2,1,0:T(8,128)S(1)}, f32[2,5,24,384]{3,2,1,0:T(8,128)}, u32[]{:S(2)}, u32[]{:S(2)}) collective-permute-start(f32[2,5,24,384]{3,2,1,0:T(8,128)S(1)} %slice.49), channel_id=1, source_target_pairs={{0,4},{1,5},{2,6},{3,7},{4,8},{5,9},{6,10},{7,11},{8,12},{9,13},{1... | collective-permute-start | bytes 1105928 | tf_op jit(solution)/shard_map/ppermute | solution.py:41
  107.5 1.9 %collective-permute-start.24 = (f32[4,5,24,384]{3,2,1,0:T(8,128)}, f32[4,5,24,384]{3,2,1,0:T(8,128)}, u32[]{:S(2)}, u32[]{:S(2)}) collective-permute-start(f32[4,5,24,384]{3,2,1,0:T(8,128)} %collective-permute-done.15.refs_6_), channel_id=1, source_target_pairs={{0,32},{1,33},{2,34},{3,35},{4,36},{5,37},{6,38},{7,39},{8,40},{9,... | collective-permute-start | bytes 2211848 | tf_op jit(solution)/shard_map/ppermute | solution.py:41
  109.4 2.4 %collective-permute-start.23 = (f32[4,5,24,384]{3,2,1,0:T(8,128)}, f32[4,5,24,384]{3,2,1,0:T(8,128)}, u32[]{:S(2)}, u32[]{:S(2)}) collective-permute-start(f32[4,5,24,384]{3,2,1,0:T(8,128)} %collective-permute-done.14.refs_5_), channel_id=1, source_target_pairs={{0,32},{1,33},{2,34},{3,35},{4,36},{5,37},{6,38},{7,39},{8,40},{9,... | collective-permute-start | bytes 2211848 | tf_op jit(solution)/shard_map/ppermute | solution.py:41
  112.1 0.1 reshape.23
  112.2 2.7 %collective-permute-start.26 = (f32[2,5,24,384]{3,2,1,0:T(8,128)}, f32[2,5,24,384]{3,2,1,0:T(8,128)}, u32[]{:S(2)}, u32[]{:S(2)}) collective-permute-start(f32[2,5,24,384]{3,2,1,0:T(8,128)} %collective-permute-done.17.refs_8_), channel_id=1, source_target_pairs={{0,32},{1,33},{2,34},{3,35},{4,36},{5,37},{6,38},{7,39},{8,40},{9,... | collective-permute-start | bytes 1105928 | tf_op jit(solution)/shard_map/ppermute | solution.py:41
  114.9 1.4 %collective-permute-done.16.refs_7_ = f32[2,5,24,384]{3,2,1,0:T(8,128)} collective-permute-done((f32[2,5,24,384]{3,2,1,0:T(8,128)S(1)}, f32[2,5,24,384]{3,2,1,0:T(8,128)}, u32[]{:S(2)}, u32[]{:S(2)}) %collective-permute-start.16) | collective-permute-done | bytes 368672 | tf_op jit(solution)/shard_map/ppermute | solution.py:41
  116.3 2.0 %collective-permute-start.25 = (f32[2,5,24,384]{3,2,1,0:T(8,128)}, f32[2,5,24,384]{3,2,1,0:T(8,128)}, u32[]{:S(2)}, u32[]{:S(2)}) collective-permute-start(f32[2,5,24,384]{3,2,1,0:T(8,128)} %collective-permute-done.16.refs_7_), channel_id=1, source_target_pairs={{0,32},{1,33},{2,34},{3,35},{4,36},{5,37},{6,38},{7,39},{8,40},{9,... | collective-permute-start | bytes 1105928 | tf_op jit(solution)/shard_map/ppermute | solution.py:41
  118.4 0.1 copy.10
  118.5 0.1 reshape.26.mask_ref
  118.7 2.2 %localize.1.local_ref = bf16[4,512,384]{2,1,0:T(8,128)(2,1)S(1)} custom-call(s32[48]{0:T(128)S(1)} %reshape.26.mask_ref, bf16[4,512,384]{2,1,0:T(8,128)(2,1)S(1)} %copy-done, bf16[384,384]{1,0:T(8,128)(2,1)S(1)} %fusion.table_ref), custom_call_target="tpu_custom_call" | custom-call | flops 603979776 | bytes 4194304 | tf_op jit(solution)/shard_map/localize/pallas_call | solution.py:198
  121.0 17.9 %ticks.1 = f32[512,768]{1,0:T(8,128)} custom-call(s32[1]{0:T(128)} %bitcast.core_ref.where_ref, f32[512,768]{1,0:T(8,128)S(1)} %copy-done.5, bf16[4,512,384]{2,1,0:T(8,128)(2,1)S(1)} %localize.1.local_ref, f32[4,5,24,384]{3,2,1,0:T(8,128)S(1)} %copy-done.2, f32[4,5,24,384]{3,2,1,0:T(8,128)S(1)} %collective-permute-done.6.refs_1_, ...), custom_call_target="tpu_custom_call" | custom-call | flops 7247757312 | bytes 16777216 | tf_op jit(solution)/shard_map/ticks/pallas_call | solution.py:287
  (48 shorter events, 0.6 us)
Async XLA Ops:
  1.1 3.1 %collective-permute-start = (f32[24,384]{1,0:T(8,128)S(1)}, f32[24,384]{1,0:T(8,128)S(1)}, u32[]{:S(2)}, u32[]{:S(2)}) collective-permute-start(f32[24,384]{1,0:T(8,128)S(1)} %get-tuple-element.12), channel_id=1, source_target_pairs={{0,32},{1,33},{2,34},{3,35},{4,36},{5,37},{6,38},{7,39},{8,40},{9,... | collective-permute-start | bytes 110600 | tf_op jit(solution)/shard_map/ppermute | solution.py:41
  4.2 7.4 %collective-permute-start.1 = (f32[2,24,384]{2,1,0:T(8,128)S(1)}, f32[2,24,384]{2,1,0:T(8,128)S(1)}, u32[]{:S(2)}, u32[]{:S(2)}) collective-permute-start(f32[2,24,384]{2,1,0:T(8,128)S(1)} %pad_maximum_fusion.2), channel_id=1, source_target_pairs={{0,64},{1,65},{2,66},{3,67},{4,68},{5,69},{6,70},{7,71},{8,72},{9,... | collective-permute-start | bytes 221192 | tf_op jit(solution)/shard_map/ppermute | solution.py:41
  9.0 6.8 %collective-permute-start.2 = (f32[24,384]{1,0:T(8,128)S(1)}, f32[24,384]{1,0:T(8,128)S(1)}, u32[]{:S(2)}, u32[]{:S(2)}) collective-permute-start(f32[24,384]{1,0:T(8,128)S(1)} %get-tuple-element.20), channel_id=1, source_target_pairs={{0,128},{1,129},{2,130},{3,131},{4,132},{5,133},{6,134},{7,135},{8... | collective-permute-start | bytes 110600 | tf_op jit(solution)/shard_map/ppermute | solution.py:41
  15.7 10.8 %collective-permute-start.5 = (f32[5,24,384]{2,1,0:T(8,128)S(1)}, f32[5,24,384]{2,1,0:T(8,128)S(1)}, u32[]{:S(2)}, u32[]{:S(2)}) collective-permute-start(f32[5,24,384]{2,1,0:T(8,128)S(1)} %bitcast_dynamic-update-slice_fusion), channel_id=1, source_target_pairs={{0,2},{1,3},{2,0},{3,1},{4,6},{5,7},{6,4},{7,5},{8,10},{9,11},{10,... | collective-permute-start | bytes 552968 | tf_op jit(solution)/shard_map/ppermute | solution.py:41
  20.7 7.4 %collective-permute-start.4 = (f32[5,24,384]{2,1,0:T(8,128)S(1)}, f32[5,24,384]{2,1,0:T(8,128)S(1)}, u32[]{:S(2)}, u32[]{:S(2)}) collective-permute-start(f32[5,24,384]{2,1,0:T(8,128)S(1)} %bitcast_dynamic-update-slice_fusion), channel_id=1, source_target_pairs={{0,3},{1,0},{2,1},{3,2},{4,7},{5,4},{6,5},{7,6},{8,11},{9,8},{10,9... | collective-permute-start | bytes 552968 | tf_op jit(solution)/shard_map/ppermute | solution.py:41
  23.7 8.6 %collective-permute-start.3 = (f32[5,24,384]{2,1,0:T(8,128)S(1)}, f32[5,24,384]{2,1,0:T(8,128)S(1)}, u32[]{:S(2)}, u32[]{:S(2)}) collective-permute-start(f32[5,24,384]{2,1,0:T(8,128)S(1)} %bitcast_dynamic-update-slice_fusion), channel_id=1, source_target_pairs={{0,1},{1,2},{2,3},{3,0},{4,5},{5,6},{6,7},{7,4},{8,9},{9,10},{10,1... | collective-permute-start | bytes 552968 | tf_op jit(solution)/shard_map/ppermute | solution.py:41
  32.4 30.6 %copy-start.1 = (f32[4,5,24,384]{3,2,1,0:T(8,128)}, f32[4,5,24,384]{3,2,1,0:T(8,128)S(1)}, u32[]{:S(2)}) copy-start(f32[4,5,24,384]{3,2,1,0:T(8,128)S(1)} %pad_maximum_fusion.refs_0_) | copy-start | bytes 2211844
  32.4 21.9 %collective-permute-start.11 = (f32[4,5,24,384]{3,2,1,0:T(8,128)S(1)}, f32[4,5,24,384]{3,2,1,0:T(8,128)S(1)}, u32[]{:S(2)}, u32[]{:S(2)}) collective-permute-start(f32[4,5,24,384]{3,2,1,0:T(8,128)S(1)} %pad_maximum_fusion.refs_0_), channel_id=1, source_target_pairs={{0,28},{1,29},{2,30},{3,31},{4,0},{5,1},{6,2},{7,3},{8,4},{9,5},{1... | collective-permute-start | bytes 2211848 | tf_op jit(solution)/shard_map/ppermute | solution.py:41
  43.4 16.5 %collective-permute-start.6 = (f32[4,5,24,384]{3,2,1,0:T(8,128)S(1)}, f32[4,5,24,384]{3,2,1,0:T(8,128)S(1)}, u32[]{:S(2)}, u32[]{:S(2)}) collective-permute-start(f32[4,5,24,384]{3,2,1,0:T(8,128)S(1)} %pad_maximum_fusion.refs_0_), channel_id=1, source_target_pairs={{0,4},{1,5},{2,6},{3,7},{4,8},{5,9},{6,10},{7,11},{8,12},{9,13},{1... | collective-permute-start | bytes 2211848 | tf_op jit(solution)/shard_map/ppermute | solution.py:41
  45.3 1.4 collective-permute-start.8
  46.0 1.4 collective-permute-start.7
  46.7 1.4 collective-permute-start.10
  47.4 0.7 collective-permute-start.9
  54.3 8.7 %copy-start.3 = (f32[4,5,24,384]{3,2,1,0:T(8,128)}, f32[4,5,24,384]{3,2,1,0:T(8,128)S(1)}, u32[]{:S(2)}) copy-start(f32[4,5,24,384]{3,2,1,0:T(8,128)S(1)} %collective-permute-done.11.refs_2_) | copy-start | bytes 2211844
  61.0 34.1 %copy-start.7 = (s32[2,32,2]{1,2,0:T(2,128)S(1)}, s32[2,32,2]{1,2,0:T(2,128)}, u32[]{:S(2)}) copy-start(s32[2,32,2]{1,2,0:T(2,128)} %constant.77.clone) | copy-start | bytes 1540
  61.0 13.6 %collective-permute-start.13 = (f32[4,5,24,384]{3,2,1,0:T(8,128)S(1)}, f32[4,5,24,384]{3,2,1,0:T(8,128)}, u32[]{:S(2)}, u32[]{:S(2)}) collective-permute-start(f32[4,5,24,384]{3,2,1,0:T(8,128)S(1)} %get-tuple-element.21), channel_id=1, source_target_pairs={{0,28},{1,29},{2,30},{3,31},{4,0},{5,1},{6,2},{7,3},{8,4},{9,5},{1... | collective-permute-start | bytes 2211848 | tf_op jit(solution)/shard_map/ppermute | solution.py:41
  63.0 55.4 %copy-start.6 = (s32[4,4,3]{1,0,2:T(4,128)S(1)}, s32[4,4,3]{1,0,2:T(4,128)}, u32[]{:S(2)}) copy-start(s32[4,4,3]{1,0,2:T(4,128)} %param.10) | copy-start | bytes 580
  63.1 55.6 %copy-start = (bf16[4,512,384]{2,1,0:T(8,128)(2,1)S(1)}, bf16[4,512,384]{2,1,0:T(8,128)(2,1)}, u32[]{:S(2)}) copy-start(bf16[4,512,384]{2,1,0:T(8,128)(2,1)} %taper_ref) | copy-start | bytes 4718596
  63.1 14.9 %collective-permute-start.12 = (f32[4,5,24,384]{3,2,1,0:T(8,128)}, f32[4,5,24,384]{3,2,1,0:T(8,128)S(1)}, u32[]{:S(2)}, u32[]{:S(2)}) collective-permute-start(f32[4,5,24,384]{3,2,1,0:T(8,128)} %get-tuple-element.22.refs_9_), channel_id=1, source_target_pairs={{0,4},{1,5},{2,6},{3,7},{4,8},{5,9},{6,10},{7,11},{8,12},{9,13},{1... | collective-permute-start | bytes 2211848 | tf_op jit(solution)/shard_map/ppermute | solution.py:41
  74.6 13.7 %collective-permute-start.15 = (f32[4,5,24,384]{3,2,1,0:T(8,128)}, f32[4,5,24,384]{3,2,1,0:T(8,128)}, u32[]{:S(2)}, u32[]{:S(2)}) collective-permute-start(f32[4,5,24,384]{3,2,1,0:T(8,128)} %collective-permute-done.13.refs_4_), channel_id=1, source_target_pairs={{0,28},{1,29},{2,30},{3,31},{4,0},{5,1},{6,2},{7,3},{8,4},{9,5},{1... | collective-permute-start | bytes 2211848 | tf_op jit(solution)/shard_map/ppermute | solution.py:41
  78.1 14.7 %collective-permute-start.14 = (f32[4,5,24,384]{3,2,1,0:T(8,128)S(1)}, f32[4,5,24,384]{3,2,1,0:T(8,128)}, u32[]{:S(2)}, u32[]{:S(2)}) collective-permute-start(f32[4,5,24,384]{3,2,1,0:T(8,128)S(1)} %broadcast_select_fusion), channel_id=1, source_target_pairs={{0,4},{1,5},{2,6},{3,7},{4,8},{5,9},{6,10},{7,11},{8,12},{9,13},{1... | collective-permute-start | bytes 2211848 | tf_op jit(solution)/shard_map/ppermute | solution.py:41
  80.8 17.1 %collective-permute-start.18 = (f32[4,5,24,384]{3,2,1,0:T(8,128)}, f32[4,5,24,384]{3,2,1,0:T(8,128)}, u32[]{:S(2)}, u32[]{:S(2)}) collective-permute-start(f32[4,5,24,384]{3,2,1,0:T(8,128)} %copy-done.1), channel_id=1, source_target_pairs={{0,32},{1,33},{2,34},{3,35},{4,36},{5,37},{6,38},{7,39},{8,40},{9,... | collective-permute-start | bytes 2211848 | tf_op jit(solution)/shard_map/ppermute | solution.py:41
  83.5 16.4 %collective-permute-start.20 = (f32[4,5,24,384]{3,2,1,0:T(8,128)}, f32[4,5,24,384]{3,2,1,0:T(8,128)}, u32[]{:S(2)}, u32[]{:S(2)}) collective-permute-start(f32[4,5,24,384]{3,2,1,0:T(8,128)} %copy-done.3), channel_id=1, source_target_pairs={{0,32},{1,33},{2,34},{3,35},{4,36},{5,37},{6,38},{7,39},{8,40},{9,... | collective-permute-start | bytes 2211848 | tf_op jit(solution)/shard_map/ppermute | solution.py:41
  85.4 20.1 %collective-permute-start.27 = (f32[4,5,24,384]{3,2,1,0:T(8,128)}, f32[4,5,24,384]{3,2,1,0:T(8,128)}, u32[]{:S(2)}, u32[]{:S(2)}) collective-permute-start(f32[4,5,24,384]{3,2,1,0:T(8,128)} %get-tuple-element.22.refs_9_), channel_id=1, source_target_pairs={{32,0},{33,1},{34,2},{35,3},{36,4},{37,5},{38,6},{39,7},{40,8},{41... | collective-permute-start | bytes 2211848 | tf_op jit(solution)/shard_map/ppermute | solution.py:41
  88.2 19.3 %collective-permute-start.19 = (f32[4,5,24,384]{3,2,1,0:T(8,128)S(1)}, f32[4,5,24,384]{3,2,1,0:T(8,128)}, u32[]{:S(2)}, u32[]{:S(2)}) collective-permute-start(f32[4,5,24,384]{3,2,1,0:T(8,128)S(1)} %collective-permute-done.6.refs_1_), channel_id=1, source_target_pairs={{0,32},{1,33},{2,34},{3,35},{4,36},{5,37},{6,38},{7,39},{8,40},{9,... | collective-permute-start | bytes 2211848 | tf_op jit(solution)/shard_map/ppermute | solution.py:41
  92.7 16.7 %collective-permute-start.22 = (f32[4,5,24,384]{3,2,1,0:T(8,128)}, f32[4,5,24,384]{3,2,1,0:T(8,128)}, u32[]{:S(2)}, u32[]{:S(2)}) collective-permute-start(f32[4,5,24,384]{3,2,1,0:T(8,128)} %collective-permute-done.13.refs_4_), channel_id=1, source_target_pairs={{0,32},{1,33},{2,34},{3,35},{4,36},{5,37},{6,38},{7,39},{8,40},{9,... | collective-permute-start | bytes 2211848 | tf_op jit(solution)/shard_map/ppermute | solution.py:41
  97.9 23.0 %collective-permute-start.21 = (f32[4,5,24,384]{3,2,1,0:T(8,128)S(1)}, f32[4,5,24,384]{3,2,1,0:T(8,128)}, u32[]{:S(2)}, u32[]{:S(2)}) collective-permute-start(f32[4,5,24,384]{3,2,1,0:T(8,128)S(1)} %collective-permute-done.12.refs_3_), channel_id=1, source_target_pairs={{0,32},{1,33},{2,34},{3,35},{4,36},{5,37},{6,38},{7,39},{8,40},{9,... | collective-permute-start | bytes 2211848 | tf_op jit(solution)/shard_map/ppermute | solution.py:41
  99.9 12.3 %collective-permute-start.17 = (f32[2,5,24,384]{3,2,1,0:T(8,128)}, f32[2,5,24,384]{3,2,1,0:T(8,128)}, u32[]{:S(2)}, u32[]{:S(2)}) collective-permute-start(f32[2,5,24,384]{3,2,1,0:T(8,128)} %slice.50), channel_id=1, source_target_pairs={{0,28},{1,29},{2,30},{3,31},{4,0},{5,1},{6,2},{7,3},{8,4},{9,5},{1... | collective-permute-start | bytes 1105928 | tf_op jit(solution)/shard_map/ppermute | solution.py:41
  105.6 10.7 %collective-permute-start.16 = (f32[2,5,24,384]{3,2,1,0:T(8,128)S(1)}, f32[2,5,24,384]{3,2,1,0:T(8,128)}, u32[]{:S(2)}, u32[]{:S(2)}) collective-permute-start(f32[2,5,24,384]{3,2,1,0:T(8,128)S(1)} %slice.49), channel_id=1, source_target_pairs={{0,4},{1,5},{2,6},{3,7},{4,8},{5,9},{6,10},{7,11},{8,12},{9,13},{1... | collective-permute-start | bytes 1105928 | tf_op jit(solution)/shard_map/ppermute | solution.py:41
  107.5 13.4 %collective-permute-start.24 = (f32[4,5,24,384]{3,2,1,0:T(8,128)}, f32[4,5,24,384]{3,2,1,0:T(8,128)}, u32[]{:S(2)}, u32[]{:S(2)}) collective-permute-start(f32[4,5,24,384]{3,2,1,0:T(8,128)} %collective-permute-done.15.refs_6_), channel_id=1, source_target_pairs={{0,32},{1,33},{2,34},{3,35},{4,36},{5,37},{6,38},{7,39},{8,40},{9,... | collective-permute-start | bytes 2211848 | tf_op jit(solution)/shard_map/ppermute | solution.py:41
  109.4 11.5 %collective-permute-start.23 = (f32[4,5,24,384]{3,2,1,0:T(8,128)}, f32[4,5,24,384]{3,2,1,0:T(8,128)}, u32[]{:S(2)}, u32[]{:S(2)}) collective-permute-start(f32[4,5,24,384]{3,2,1,0:T(8,128)} %collective-permute-done.14.refs_5_), channel_id=1, source_target_pairs={{0,32},{1,33},{2,34},{3,35},{4,36},{5,37},{6,38},{7,39},{8,40},{9,... | collective-permute-start | bytes 2211848 | tf_op jit(solution)/shard_map/ppermute | solution.py:41
  112.2 8.7 %collective-permute-start.26 = (f32[2,5,24,384]{3,2,1,0:T(8,128)}, f32[2,5,24,384]{3,2,1,0:T(8,128)}, u32[]{:S(2)}, u32[]{:S(2)}) collective-permute-start(f32[2,5,24,384]{3,2,1,0:T(8,128)} %collective-permute-done.17.refs_8_), channel_id=1, source_target_pairs={{0,32},{1,33},{2,34},{3,35},{4,36},{5,37},{6,38},{7,39},{8,40},{9,... | collective-permute-start | bytes 1105928 | tf_op jit(solution)/shard_map/ppermute | solution.py:41
  116.3 4.6 %collective-permute-start.25 = (f32[2,5,24,384]{3,2,1,0:T(8,128)}, f32[2,5,24,384]{3,2,1,0:T(8,128)}, u32[]{:S(2)}, u32[]{:S(2)}) collective-permute-start(f32[2,5,24,384]{3,2,1,0:T(8,128)} %collective-permute-done.16.refs_7_), channel_id=1, source_target_pairs={{0,32},{1,33},{2,34},{3,35},{4,36},{5,37},{6,38},{7,39},{8,40},{9,... | collective-permute-start | bytes 1105928 | tf_op jit(solution)/shard_map/ppermute | solution.py:41
  118.6 2.3 %copy-start.2 = (f32[4,5,24,384]{3,2,1,0:T(8,128)S(1)}, f32[4,5,24,384]{3,2,1,0:T(8,128)}, u32[]{:S(2)}) copy-start(f32[4,5,24,384]{3,2,1,0:T(8,128)} %copy-done.1) | copy-start | bytes 2211844
  118.6 2.3 %copy-start.4 = (f32[4,5,24,384]{3,2,1,0:T(8,128)S(1)}, f32[4,5,24,384]{3,2,1,0:T(8,128)}, u32[]{:S(2)}) copy-start(f32[4,5,24,384]{3,2,1,0:T(8,128)} %copy-done.3) | copy-start | bytes 2211844
  118.7 2.3 %copy-start.5 = (f32[512,768]{1,0:T(8,128)S(1)}, f32[512,768]{1,0:T(8,128)}, u32[]{:S(2)}) copy-start(f32[512,768]{1,0:T(8,128)} %state_ref.1) | copy-start | bytes 4718596
